TPU v7x, 128 devices: a whole 4x4x4 slice. The times are simulated.
128 devices in a mesh: wide: 16 (over z, x), narrow: 8 (over y, core).
Axes of the slice: x: 4, y: 4, z: 4, core: 2. Of those that a mesh axis runs over, the one named last changes fastest.
Arguments:
- tokens: bfloat16 [6144, 2560], P(('wide', 'narrow')), may hold values from -6 to 6
- scores: float32 [6144], P(('wide', 'narrow')), may hold values from 0.25 to 1
- expert_ids: int32 [6144], P(('wide', 'narrow')), may hold values from 0 to 63, as said below
- gate_halves: bfloat16 [128, 2560, 2048], P(('wide', 'narrow')), may hold values from -0.125 to 0.125
- up_halves: bfloat16 [128, 2560, 2048], P(('wide', 'narrow')), may hold values from -0.125 to 0.125
- shared_gate: bfloat16 [2560, 4096], P(None, 'narrow'), may hold values from -0.125 to 0.125
- shared_up: bfloat16 [2560, 4096], P(None, 'narrow'), may hold values from -0.125 to 0.125
Outputs:
- routed_hidden: bfloat16 [6144, 4096], P(('wide', 'narrow'))
- shared_hidden: bfloat16 [6144, 4096], P('wide', 'narrow')
Inputs may be any that keep to these rules, and one draw needn't show every extreme that they name: `expert_ids`: within the 48 rows of each device no expert is named more than 2 times, and one expert, the same for every device, is named exactly 2 times in the rows of every device.
All inputs are finite; a program needn't handle non-finite values.
Results may differ from a plain program's by a relative error of at most 0.0058.
Values may be sent and summed in bfloat16 or wider, within the bound.
No kernel may reach another device: no remote copies, remote signals or barrier semaphores. Data moves between devices by JAX's collectives and lax.ppermute only.
A program may use at most 128 MiB of HBM per device.

v0:
```python
import jax
import jax.numpy as jnp
from jax import lax
from jax.sharding import PartitionSpec as P

CAP = 2


def swiglu_rows(inputs, gate_matrix, up_matrix):
    gate_val = jnp.dot(inputs, gate_matrix, preferred_element_type=jnp.float32)
    up_val = jnp.dot(inputs, up_matrix, preferred_element_type=jnp.float32)
    return (jax.nn.silu(gate_val) * up_val).astype(jnp.bfloat16)


def select_rows(onehot, table):
    return jnp.dot(onehot.astype(jnp.bfloat16), table, preferred_element_type=jnp.float32).astype(
        jnp.bfloat16
    )


def shards(tokens, scores, expert_ids, gate_halves, up_halves, shared_gate, shared_up):
    rows_here = tokens.shape[0]
    width = tokens.shape[1]
    half_units = gate_halves.shape[2]
    devices = lax.axis_size(("wide", "narrow"))
    gate_mine = gate_halves[0]
    up_mine = up_halves[0]
    shared_hidden = swiglu_rows(
        lax.all_gather(tokens, "narrow", axis=0, tiled=True), shared_gate, shared_up
    )
    scaled = (tokens.astype(jnp.float32) * scores[:, None]).astype(jnp.bfloat16)
    position = jnp.arange(rows_here, dtype=jnp.int32)
    earlier = (expert_ids[:, None] == expert_ids[None, :]) & (position[None, :] < position[:, None])
    rank = jnp.sum(earlier.astype(jnp.int32), axis=1)
    slots = CAP
    entry_first = 2 * expert_ids * slots + rank
    entry_second = (2 * expert_ids + 1) * slots + rank
    cells = jnp.arange(devices * slots, dtype=jnp.int32)
    place_table = (cells[:, None] == entry_first[None, :]) | (
        cells[:, None] == entry_second[None, :]
    )
    outgoing = select_rows(place_table, scaled).reshape(devices, slots, width)
    received = lax.all_to_all(outgoing, ("wide", "narrow"), split_axis=0, concat_axis=0, tiled=True)
    count = received.shape[1]
    flat = received.reshape(devices * count, width)
    returned = lax.all_to_all(
        swiglu_rows(flat, gate_mine, up_mine).reshape(devices, count, half_units),
        ("wide", "narrow"),
        split_axis=0,
        concat_axis=0,
        tiled=True,
    )
    returned_flat = returned.reshape(devices * slots, returned.shape[2])
    first_pick = cells[None, :] == entry_first[:, None]
    second_pick = cells[None, :] == entry_second[:, None]
    routed_hidden = jnp.concatenate(
        [select_rows(first_pick, returned_flat), select_rows(second_pick, returned_flat)], axis=1
    )
    return (routed_hidden, shared_hidden)


def solution(mesh):
    placed = (
        P(("wide", "narrow"), None),
        P(("wide", "narrow")),
        P(("wide", "narrow")),
        P(("wide", "narrow"), None, None),
        P(("wide", "narrow"), None, None),
        P(None, "narrow"),
        P(None, "narrow"),
    )
    return jax.shard_map(
        shards,
        mesh=mesh,
        in_specs=placed,
        out_specs=(P(("wide", "narrow"), None), P("wide", "narrow")),
        check_vma=False,
    )
```

profile of v0, /device:TPU:1, one launch (start us, length us, event | category | flops | bytes accessed | tf_op | source)
XLA Modules:
  0.0 113.5 jit_solution(14014924160276387807)
XLA Ops:
  7.2 0.0 copy-start
  7.2 1.0 convert_reduce_fusion
  8.2 0.7 multiply_add_fusion.1
  8.8 2.6 %convolution_convert_fusion = bf16[256,2560]{1,0:T(8,128)(2,1)} fusion(bf16[48,2560]{1,0:T(8,128)(2,1)} %param.7, f32[48]{0:T(128)} %param.8, s32[48]{0:T(128)S(1)} %get-tuple-element.3, s32[48]{0:T(128)S(1)} %get-tuple-element.2), kind=kOutput, calls=%fused_computation.4 | convolution fusion | flops 63975424 | bytes 1557056 | tf_op jit(solution)/shard_map/dot_general | solution.py:16
  11.4 4.0 %reshape.23 = bf16[128,2,2560]{2,1,0:T(2,128)(2,1)} reshape(bf16[256,2560]{1,0:T(8,128)(2,1)} %convolution_convert_fusion) | data formatting | bytes 2621440 | tf_op jit(solution)/shard_map/reshape | solution.py:42
  15.4 11.9 %all-to-all-start = ((bf16[128,2,2560]{2,1,0:T(2,128)(2,1)}), bf16[128,2,2560]{2,1,0:T(2,128)(2,1)}, u32[]{:S(2)}, u32[]{:S(2)}) async-start(bf16[128,2,2560]{2,1,0:T(2,128)(2,1)} %reshape.23), calls=%async_computation | async-start | bytes 2621440 | tf_op jit(solution)/shard_map/all_to_all | solution.py:43
  27.3 0.0 all-gather.2.cloned.1.call-start
  27.4 0.7 all-gather.2.cloned.1.call-update
  28.0 20.6 %all-to-all-done = bf16[128,2,2560]{2,1,0:T(2,128)(2,1)} async-done(((bf16[128,2,2560]{2,1,0:T(2,128)(2,1)}), bf16[128,2,2560]{2,1,0:T(2,128)(2,1)}, u32[]{:S(2)}, u32[]{:S(2)}) %all-to-all-start) | async-done | bytes 1310752 | tf_op jit(solution)/shard_map/all_to_all | solution.py:43
  48.7 4.1 %reshape.24 = bf16[256,2560]{1,0:T(8,128)(2,1)} reshape(bf16[128,2,2560]{2,1,0:T(2,128)(2,1)} %all-to-all-done) | data formatting | bytes 2621440 | tf_op jit(solution)/shard_map/reshape | solution.py:45
  52.8 7.2 %fusion.2 = f32[256,2048]{1,0:T(8,128)S(1)} fusion(bf16[256,2560]{1,0:T(8,128)(2,1)} %reshape.24, bf16[1,2560,2048]{2,1,0:T(8,128)(2,1)} %param.10), kind=kOutput, calls=%fused_computation.2 | convolution fusion | flops 2684354560 | bytes 13893632 | tf_op jit(solution)/shard_map/dot_general | solution.py:10
  60.0 0.0 copy-done.1
  60.0 8.4 %fusion.7 = bf16[256,2048]{1,0:T(8,128)(2,1)} fusion(bf16[256,2560]{1,0:T(8,128)(2,1)S(1)} %copy-done.1, bf16[1,2560,2048]{2,1,0:T(8,128)(2,1)} %param.11, f32[256,2048]{1,0:T(8,128)S(1)} %fusion.2), kind=kOutput, calls=%fused_computation.6 | convolution fusion | flops 2687500288 | bytes 14942208 | tf_op jit(solution)/shard_map/dot_general | solution.py:11
  68.4 2.5 %reshape.25 = bf16[128,2,2048]{2,1,0:T(2,128)(2,1)} reshape(bf16[256,2048]{1,0:T(8,128)(2,1)} %fusion.7) | data formatting | bytes 2097152 | tf_op jit(solution)/shard_map/reshape | solution.py:47
  70.9 24.7 %all_to_all.10 = bf16[128,2,2048]{2,1,0:T(2,128)(2,1)} all-to-all(bf16[128,2,2048]{2,1,0:T(2,128)(2,1)} %reshape.25), channel_id=1, replica_groups=mesh['wide'=16,'narrow'=8] {'wide','narrow'}, dimensions={0} | all-to-all | bytes 2097152 | tf_op jit(solution)/shard_map/all_to_all | solution.py:46
  95.6 2.3 %reshape.26 = bf16[256,2048]{1,0:T(8,128)(2,1)} reshape(bf16[128,2,2048]{2,1,0:T(2,128)(2,1)} %all_to_all.10) | data formatting | bytes 2097152 | tf_op jit(solution)/shard_map/reshape | solution.py:53
  97.9 1.5 %convolution_convert_fusion.2 = bf16[48,2048]{1,0:T(8,128)(2,1)S(1)} fusion(bf16[256,2048]{1,0:T(8,128)(2,1)} %reshape.26, s32[48]{0:T(128)S(1)} %get-tuple-element.2), kind=kOutput, calls=%fused_computation.8 | convolution fusion | flops 50442240 | bytes 1245376 | tf_op jit(solution)/shard_map/dot_general | solution.py:16
  99.4 1.6 %convolution_convert_fusion.1 = bf16[48,2048]{1,0:T(8,128)(2,1)S(1)} fusion(bf16[256,2048]{1,0:T(8,128)(2,1)} %reshape.26, s32[48]{0:T(128)S(1)} %get-tuple-element.3), kind=kOutput, calls=%fused_computation.7 | convolution fusion | flops 50442240 | bytes 1245376 | tf_op jit(solution)/shard_map/dot_general | solution.py:16
  101.0 0.8 pad_maximum_fusion
  101.8 0.0 copy-done
  101.8 2.9 %fusion.19 = f32[384,512]{1,0:T(8,128)S(1)} fusion(bf16[384,2560]{1,0:T(8,128)(2,1)} %all-gather.2.cloned.1.call-done, bf16[2560,512]{1,0:T(8,128)(2,1)S(1)} %copy-done), kind=kOutput, calls=%fused_computation.28 | convolution fusion | flops 1006632960 | bytes 5373952 | tf_op jit(solution)/shard_map/dot_general | solution.py:10
  104.7 0.0 copy-done.2
  104.7 0.0 copy-done.3
  104.7 2.0 %fusion.10 = bf16[384,512]{1,0:T(8,128)(2,1)} fusion(bf16[384,2560]{1,0:T(8,128)(2,1)S(1)} %copy-done.3, bf16[2560,512]{1,0:T(8,128)(2,1)S(1)} %copy-done.2, f32[384,512]{1,0:T(8,128)S(1)} %fusion.19), kind=kOutput, calls=%fused_computation.10 | convolution fusion | flops 1007812608 | bytes 5767168 | tf_op jit(solution)/shard_map/dot_general | solution.py:11
  (4 shorter events, 0.0 us)
Async XLA Ops:
  7.2 94.6 %copy-start = (bf16[2560,512]{1,0:T(8,128)(2,1)S(1)}, bf16[2560,512]{1,0:T(8,128)(2,1)}, u32[]{:S(2)}) copy-start(bf16[2560,512]{1,0:T(8,128)(2,1)} %param.12) | copy-start | bytes 7864324
  15.4 33.3 %all-to-all-start = ((bf16[128,2,2560]{2,1,0:T(2,128)(2,1)}), bf16[128,2,2560]{2,1,0:T(2,128)(2,1)}, u32[]{:S(2)}, u32[]{:S(2)}) async-start(bf16[128,2,2560]{2,1,0:T(2,128)(2,1)} %reshape.23), calls=%async_computation | async-start | bytes 2621440 | tf_op jit(solution)/shard_map/all_to_all | solution.py:43
  27.3 74.5 %all-gather.2.cloned.1.call-start = ((), (), s32[]{:S(2)}) async-start(), calls=%async_computation.2 | async-start | bytes 2211840 | tf_op jit(solution)/shard_map/all_gather | solution.py:29
  52.8 7.2 %copy-start.1 = (bf16[256,2560]{1,0:T(8,128)(2,1)S(1)}, bf16[256,2560]{1,0:T(8,128)(2,1)}, u32[]{:S(2)}) copy-start(bf16[256,2560]{1,0:T(8,128)(2,1)} %reshape.24) | copy-start | bytes 3932164
  101.8 2.9 %copy-start.2 = (bf16[2560,512]{1,0:T(8,128)(2,1)S(1)}, bf16[2560,512]{1,0:T(8,128)(2,1)}, u32[]{:S(2)}) copy-start(bf16[2560,512]{1,0:T(8,128)(2,1)} %param.13) | copy-start | bytes 7864324
  101.8 2.9 %copy-start.3 = (bf16[384,2560]{1,0:T(8,128)(2,1)S(1)}, bf16[384,2560]{1,0:T(8,128)(2,1)}, u32[]{:S(2)}) copy-start(bf16[384,2560]{1,0:T(8,128)(2,1)} %all-gather.2.cloned.1.call-done) | copy-start | bytes 5898244
Sparse Core Ops, SparseCore 0:
  29.8 27.6 all-gather.1
where the time goes:
time: 114 us
  matrix products  26.1 us (23%)
  blocking collectives  24.7 us (22%)
  waiting for transfers between devices  21.3 us (19%)
  between operations  14.1 us (12%)
  local copies, waits for them, and re-layouts  12.9 us (11%)
  starting transfers between devices  11.9 us (10%)
  other arithmetic  2.44 us (2%)
    all_to_all x1, blocking collectives, shards(): lax.all_to_all(swiglu_rows(flat, gate_mine, up_mine).reshape(devices, cou...  24.7 us
    all_to_all x1, waiting for transfers between devices, shards(): lax.all_to_all(outgoing, ('wide', 'narrow'), split_axis=0, concat_axis=0,...  20.6 us
    all_to_all x1, starting transfers between devices, shards(): lax.all_to_all(outgoing, ('wide', 'narrow'), split_axis=0, concat_axis=0,...  11.9 us
    dot_general x2, matrix products, swiglu_rows(): up_val = jnp.dot(inputs, up_matrix, preferred_element_type=jnp.float32)  10.3 us
    dot_general x2, matrix products, swiglu_rows(): gate_val = jnp.dot(inputs, gate_matrix, preferred_element_type=jnp.float32)  10.1 us
    dot_general x3, matrix products, select_rows(): jnp.dot(onehot.astype(jnp.bfloat16), table, preferred_element_type=jnp.fl...  5.69 us
    reshape x1, local copies, waits for them, and re-layouts, shards(): flat = received.reshape(devices * count, width)  4.1 us
    reshape x1, local copies, waits for them, and re-layouts, shards(): outgoing = select_rows(place_table, scaled).reshape(devices, slots, width)  3.96 us
  transfers between devices with their start and end apart: 2, of which 1 were waited for; matrix products, arithmetic and copies ran while one was open for 25% of the time, Pallas kernels for 0%

commit v1 on v0

v1 whole, which is shorter than its diff:
```python
import jax
import jax.numpy as jnp
from jax import lax
from jax.experimental import pallas as pl
from jax.experimental.pallas import tpu as pltpu
from jax.sharding import Mesh, PartitionSpec as P

CAP = 2
LANES = 128
TILE = 256
STAGED = 3
F32 = jnp.float32
BF16 = jnp.bfloat16
I32 = jnp.int32


def iota(shape, dim):
    return lax.broadcasted_iota(I32, shape, dim)


def column(row, n):
    eye = iota((n, n), 0) == iota((n, n), 1)
    return jnp.sum(jnp.where(eye, jnp.broadcast_to(row, (n, n)), 0), axis=1, keepdims=True)


def dispatch_kernel(tokens_ref, scores_ref, ids_ref, send_ref):
    n, width = tokens_ref.shape
    pieces = 8 // CAP
    part = width // pieces
    ids_row = ids_ref[...].reshape(1, n)
    ids_col = column(ids_row, n)
    score_col = column(scores_ref[...].reshape(1, n), n)
    tokens = tokens_ref[...]
    scaled = (tokens.astype(F32) * score_col).astype(BF16)
    earlier = (ids_col == ids_row) & (iota((n, n), 0) < iota((n, n), 1))
    rank_row = jnp.sum(earlier.astype(I32), axis=0, keepdims=True)
    entry = 8 * ids_row + pieces * rank_row
    rows = iota((send_ref.shape[0], n), 0)
    hot = jnp.concatenate(
        [(rows == entry + j).astype(F32).astype(BF16) for j in range(pieces)], axis=1
    )
    stack = jnp.concatenate([scaled[:, j * part : (j + 1) * part] for j in range(pieces)], axis=0)
    send_ref[...] = jnp.dot(hot, stack, preferred_element_type=F32).astype(BF16)


def dispatch(tokens, scores, expert_ids, chips):
    n, width = tokens.shape
    return pl.pallas_call(
        dispatch_kernel,
        out_shape=jax.ShapeDtypeStruct((chips * 8, width * CAP // 8), BF16),
        compiler_params=pltpu.CompilerParams(vmem_limit_bytes=60 << 20),
        name="dispatch",
        cost_estimate=pl.CostEstimate(flops=10**8, bytes_accessed=2 * 10**6, transcendentals=0),
    )(tokens, scores, expert_ids)


def silu_mul(gate, up):
    return gate / (1.0 + jnp.exp(-gate)) * up


def tiles(units):
    pieces = 8 // CAP
    return [(q, j) for q in range(units // pieces // TILE) for j in range(pieces)]


def tile_of(ref, q, j):
    start = j * (ref.shape[1] * CAP // 8) + q * TILE
    return ref.at[:, start : start + TILE]


def stage_kernel(gate_ref, up_ref, gate_out, up_out, sems):
    copies = []
    for i, (q, j) in enumerate(tiles(gate_ref.shape[1])[: gate_out.shape[0]]):
        copies.append(pltpu.make_async_copy(tile_of(gate_ref, q, j), gate_out.at[i], sems.at[0, i]))
        copies.append(pltpu.make_async_copy(tile_of(up_ref, q, j), up_out.at[i], sems.at[1, i]))
    for copy in copies:
        copy.start()
    for copy in copies:
        copy.wait()


def stage(gate, up, count):
    shape = (count, gate.shape[0], TILE)
    return pl.pallas_call(
        stage_kernel,
        out_shape=(pltpu.VMEM(shape, BF16), pltpu.VMEM(shape, BF16)),
        in_specs=[pl.BlockSpec(memory_space=pltpu.HBM)] * 2,
        out_specs=(pl.BlockSpec(memory_space=pltpu.VMEM),) * 2,
        scratch_shapes=[pltpu.SemaphoreType.DMA((2, count))],
        compiler_params=pltpu.CompilerParams(vmem_limit_bytes=1 << 20),
        name="stage",
        cost_estimate=pl.CostEstimate(flops=0, bytes_accessed=10**7, transcendentals=0),
    )(gate, up)


def routed_kernel(
    own_ref, other_ref, gate_ref, up_ref, gate_first, up_first, out_ref, rows_ref, hidden_ref,
    gate_rest, up_rest, sems,
):
    core = lax.axis_index("core")
    chips = own_ref.shape[0] // 8
    part = own_ref.shape[1]
    pieces = 8 // CAP
    order = tiles(gate_ref.shape[1])
    first = gate_first.shape[0]
    copies = []
    for i, (q, j) in enumerate(order[first:]):
        copies.append(
            (
                pltpu.make_async_copy(tile_of(gate_ref, q, j), gate_rest.at[i], sems.at[0, i]),
                pltpu.make_async_copy(tile_of(up_ref, q, j), up_rest.at[i], sems.at[1, i]),
            )
        )
    for pair in copies:
        for copy in pair:
            copy.start()
    to = iota((8 * chips, 8 * chips), 0)
    at = 8 * (to % chips) + pieces * (to // chips % CAP) + to // (CAP * chips)
    perm = (iota((8 * chips, 8 * chips), 1) == at).astype(F32).astype(BF16)
    for c, ref in enumerate((own_ref, other_ref)):
        moved = jnp.dot(perm, ref[...], preferred_element_type=F32).astype(BF16)
        at = CAP * chips * c
        for j in range(pieces):
            rows_ref[at : at + CAP * chips, j * part : (j + 1) * part] = moved[
                j * CAP * chips : (j + 1) * CAP * chips
            ]
    for i, (q, j) in enumerate(order):
        if i < first:
            gate_tile, up_tile = gate_first.at[i], up_first.at[i]
        else:
            gate_tile, up_tile = gate_rest.at[i - first], up_rest.at[i - first]
            for copy in copies[i - first]:
                copy.wait()
        gate = jnp.dot(rows_ref[...], gate_tile[...], preferred_element_type=F32)
        up = jnp.dot(rows_ref[...], up_tile[...], preferred_element_type=F32)
        hidden = silu_mul(gate, up)
        for c in range(2):
            core_of = core if c == 0 else 1 - core
            for s in range(CAP):
                at = chips * (CAP * c + s)
                for k in range(TILE // LANES):
                    hidden_ref[k, pl.ds(8 * core_of + pieces * s + j, chips, stride=16), :] = (
                        hidden[at : at + chips, k * LANES : (k + 1) * LANES]
                    )
        if j == pieces - 1:
            for k in range(TILE // LANES):
                lane = q * TILE + k * LANES
                out_ref[:, lane : lane + LANES] = hidden_ref[k].astype(BF16)


def routed(own, other, gate, up, gate_first, up_first):
    rows, part = own.shape
    width, units = gate.shape
    pieces = 8 // CAP
    chips = rows // 8
    rest = units // TILE - gate_first.shape[0]
    vmem = pl.BlockSpec(memory_space=pltpu.VMEM)
    hbm = pl.BlockSpec(memory_space=pltpu.HBM)
    return pl.pallas_call(
        routed_kernel,
        out_shape=jax.ShapeDtypeStruct((16 * chips, units // pieces), BF16),
        in_specs=[vmem, vmem, hbm, hbm, vmem, vmem],
        out_specs=vmem,
        scratch_shapes=[
            pltpu.VMEM((4 * chips, width), BF16),
            pltpu.VMEM((TILE // LANES, 16 * chips, LANES), F32),
            pltpu.VMEM((rest, width, TILE), BF16),
            pltpu.VMEM((rest, width, TILE), BF16),
            pltpu.SemaphoreType.DMA((2, rest)),
        ],
        compiler_params=pltpu.CompilerParams(vmem_limit_bytes=36 << 20),
        name="routed",
        cost_estimate=pl.CostEstimate(
            flops=4 * 4 * chips * width * units, bytes_accessed=10**6, transcendentals=0
        ),
    )(own, other, gate, up, gate_first, up_first)


def shared_kernel(*refs):
    gate_ref, up_ref, out_ref = refs[-3:]
    blocks = refs[:-3]
    core = lax.axis_index("core")
    y = lax.axis_index("y")
    ring = len(blocks) // 2
    n = blocks[0].shape[0]
    for c in range(2):
        rows = jnp.concatenate([ref[...] for ref in blocks[ring * c : ring * (c + 1)]], axis=0)
        gate = jnp.dot(rows, gate_ref[...], preferred_element_type=F32)
        up = jnp.dot(rows, up_ref[...], preferred_element_type=F32)
        hidden = silu_mul(gate, up).astype(BF16)
        core_of = core if c == 0 else 1 - core
        step = 1 - 2 * core_of
        for i, back in enumerate((0, 1, -1, 2)):
            from_y = lax.rem(y - back * step + 2 * ring, ring)
            at = pl.multiple_of(n * (2 * from_y + core_of), 16)
            out_ref[pl.ds(at, n), :] = hidden[n * i : n * (i + 1)]


def shared(blocks, shared_gate, shared_up):
    n, width = blocks[0].shape
    units = shared_gate.shape[1]
    tile = 256
    whole = pl.BlockSpec((n, width), lambda q: (0, 0))
    weight = pl.BlockSpec((width, tile), lambda q: (0, q))
    return pl.pallas_call(
        shared_kernel,
        out_shape=jax.ShapeDtypeStruct((len(blocks) * n, units), BF16),
        grid=(units // tile,),
        in_specs=[whole] * len(blocks) + [weight, weight],
        out_specs=pl.BlockSpec((len(blocks) * n, tile), lambda q: (0, q)),
        compiler_params=pltpu.CompilerParams(vmem_limit_bytes=32 << 20),
        name="shared",
        cost_estimate=pl.CostEstimate(
            flops=4 * len(blocks) * n * width * units, bytes_accessed=8 * 10**6, transcendentals=0
        ),
    )(*blocks, shared_gate, shared_up)


def collect_kernel(back_ref, ids_ref, out_ref):
    n = out_ref.shape[0]
    pieces = 8 // CAP
    part = back_ref.shape[1]
    ids_row = ids_ref[...].reshape(1, n)
    ids_col = column(ids_row, n)
    earlier = (ids_col == ids_row) & (iota((n, n), 1) < iota((n, n), 0))
    rank_col = jnp.sum(earlier.astype(I32), axis=1, keepdims=True)
    entry = 16 * ids_col + pieces * rank_col
    cells = iota((n, back_ref.shape[0]), 1)
    hot = jnp.concatenate(
        [
            (cells == entry + (8 * h + j)).astype(F32).astype(BF16)
            for h in range(2)
            for j in range(pieces)
        ],
        axis=0,
    )
    picked = jnp.dot(hot, back_ref[...], preferred_element_type=F32).astype(BF16)
    for q in range(2 * pieces):
        out_ref[:, q * part : (q + 1) * part] = picked[q * n : (q + 1) * n]


def collect(back, expert_ids):
    rows, part = back.shape
    n = expert_ids.shape[0]
    return pl.pallas_call(
        collect_kernel,
        out_shape=jax.ShapeDtypeStruct((n, 8 * part), BF16),
        compiler_params=pltpu.CompilerParams(vmem_limit_bytes=8 << 20),
        name="collect",
        cost_estimate=pl.CostEstimate(flops=4 * 10**8, bytes_accessed=15 * 10**5, transcendentals=0),
    )(back, expert_ids)


def swap(x):
    return lax.ppermute(x, "core", [(0, 1), (1, 0)])


def turn(x, ring, step):
    pairs = [
        (2 * y + c, 2 * ((y + step * (1 - 2 * c)) % ring) + c) for y in range(ring) for c in range(2)
    ]
    return lax.ppermute(x, ("y", "core"), pairs)


def shards(tokens, scores, expert_ids, gate_halves, up_halves, shared_gate, shared_up):
    ring = lax.axis_size("y")
    chips = lax.axis_size("wide") * ring
    send = dispatch(tokens, scores, expert_ids, chips)
    arrived = lax.all_to_all(
        send.reshape(chips, 8, send.shape[1]), ("wide", "y"), split_axis=0, concat_axis=0, tiled=True
    ).reshape(send.shape)
    after = turn(tokens, ring, 1)
    gate = pltpu.with_memory_space_constraint(gate_halves[0], pltpu.HBM)
    up = pltpu.with_memory_space_constraint(up_halves[0], pltpu.HBM)
    arrived, after, gate, up = lax.optimization_barrier((arrived, after, gate, up))
    before = turn(tokens, ring, -1)
    opposite = turn(after, ring, 1)
    arrived_other = swap(arrived)
    gate_first, up_first = stage(gate, up, STAGED)
    hidden = routed(arrived, arrived_other, gate, up, gate_first, up_first)
    hidden, before, opposite = lax.optimization_barrier((hidden, before, opposite))
    back = lax.all_to_all(
        hidden.reshape(2 * chips, 8, hidden.shape[1]),
        ("wide", "y", "core"),
        split_axis=0,
        concat_axis=0,
        tiled=True,
    ).reshape(hidden.shape)
    blocks = [tokens, after, before, opposite]
    blocks = blocks + [swap(block) for block in blocks]
    blocks = lax.optimization_barrier((*blocks, hidden))[:-1]
    shared_hidden = shared(blocks, shared_gate, shared_up)
    back, shared_hidden = lax.optimization_barrier((back, shared_hidden))
    return collect(back, expert_ids), shared_hidden


def solution(mesh):
    wide, narrow = mesh.devices.shape
    fine = Mesh(mesh.devices.reshape(wide, narrow // 2, 2), ("wide", "y", "core"))
    every = ("wide", "y", "core")
    placed = (
        P(every, None),
        P(every),
        P(every),
        P(every, None, None),
        P(every, None, None),
        P(None, ("y", "core")),
        P(None, ("y", "core")),
    )
    return jax.shard_map(
        shards,
        mesh=fine,
        in_specs=placed,
        out_specs=(P(every, None), P("wide", ("y", "core"))),
        check_vma=False,
    )
```

time: 114 us -> 73.1 us (0.64)
  matrix products: 26.1 us -> 0 us
  blocking collectives: 24.7 us -> 0 us
  Pallas kernels: 0 us -> 22.1 us
  starting transfers between devices: 11.9 us -> 26.7 us
  between operations: 14.1 us -> 0.73 us
  local copies, waits for them, and re-layouts: 12.9 us -> 1.76 us
  other arithmetic: 2.44 us -> 0 us
    dot_general x7 -> x0, matrix products: 26.1 us -> none  [the longest x2 10.3 us: swiglu_rows(): up_val = jnp.dot(inputs, up_matrix, preferred_element_type=jnp.float32)]
    all_to_all x1 -> x0, blocking collectives: 24.7 us -> none  [shards(): lax.all_to_all(swiglu_rows(flat, gate_mine, up_mine).reshape(devices, cou...]
    pallas_call x0 -> x5, Pallas kernels: none -> 22.1 us  [the longest x1 9.12 us: routed(): pl.pallas_call(routed_kernel, out_shape=jax.ShapeDtypeStruct((16 * chips,...]
    reshape x4 -> x0, local copies, waits for them, and re-layouts: 12.9 us -> none  [the longest x1 4.1 us: shards(): flat = received.reshape(devices * count, width)]
    ppermute x0 -> x8, waiting for transfers between devices: none -> 11.4 us  [the longest x3 9.58 us: turn(): return lax.ppermute(x, ('y', 'core'), pairs)]
    all_to_all x1 -> x2, waiting for transfers between devices: 20.6 us -> 10 us  [the longest x1 8.65 us: shards(): lax.all_to_all(hidden.reshape(2 * chips, 8, hidden.shape[1]), ('wide', 'y...]
    ppermute x0 -> x8, starting transfers between devices: none -> 9.18 us  [the longest x3 4.97 us: turn(): return lax.ppermute(x, ('y', 'core'), pairs)]
    all_to_all x1 -> x2, starting transfers between devices: 11.9 us -> 17.6 us  [the longest x1 12 us: shards(): lax.all_to_all(send.reshape(chips, 8, send.shape[1]), ('wide', 'y'), spli...]
  transfers between devices with their start and end apart: 2 -> 10, of which waited for: 1 -> 7; matrix products, arithmetic and copies ran while one was open for 25% -> 0% of each run, Pallas kernels for 0% -> 23%
where the time goes in v1:
time: 73.1 us; the launch traced here: 72.7 us
  starting transfers between devices  26.7 us (37%)
  Pallas kernels  22.1 us (30%)
  waiting for transfers between devices  21.4 us (29%)
  local copies, waits for them, and re-layouts  1.76 us (2%)
    all_to_all x1, starting transfers between devices, shards(): lax.all_to_all(send.reshape(chips, 8, send.shape[1]), ('wide', 'y'), spli...  12 us
    ppermute x3, waiting for transfers between devices, turn(): return lax.ppermute(x, ('y', 'core'), pairs)  9.58 us
    pallas_call x1, Pallas kernels, routed(): pl.pallas_call(routed_kernel, out_shape=jax.ShapeDtypeStruct((16 * chips,...  9.12 us
    all_to_all x1, waiting for transfers between devices, shards(): lax.all_to_all(hidden.reshape(2 * chips, 8, hidden.shape[1]), ('wide', 'y...  8.65 us
    all_to_all x1, starting transfers between devices, shards(): lax.all_to_all(hidden.reshape(2 * chips, 8, hidden.shape[1]), ('wide', 'y...  5.59 us
    ppermute x3, starting transfers between devices, turn(): return lax.ppermute(x, ('y', 'core'), pairs)  4.97 us
    pallas_call x1, Pallas kernels, shared(): pl.pallas_call(shared_kernel, out_shape=jax.ShapeDtypeStruct((len(blocks)...  4.5 us
    ppermute x5, starting transfers between devices, swap(): return lax.ppermute(x, 'core', [(0, 1), (1, 0)])  4.21 us
  transfers between devices with their start and end apart: 10, of which 7 were waited for; matrix products, arithmetic and copies ran while one was open for 0% of the time, Pallas kernels for 23%

profile of v1, /device:TPU:1, one launch (start us, length us, event | category | flops | bytes accessed | tf_op | source)
XLA Modules:
  0.0 72.7 jit_solution(15035432894732827651)
XLA Ops:
  0.6 2.4 %dispatch.1 = bf16[512,640]{1,0:T(8,128)(2,1)} custom-call(bf16[48,2560]{1,0:T(8,128)(2,1)} %refs_0_, f32[48]{0:T(128)} %scores_ref.1, s32[48]{0:T(128)} %ids_ref.3), custom_call_target="tpu_custom_call" | custom-call | flops 100000000 | bytes 2000000 | tf_op jit(solution)/shard_map/dispatch/pallas_call | solution.py:48
  3.0 12.0 %all-to-all-start = ((bf16[64,8,640]{2,1,0:T(8,128)(2,1)}), bf16[64,8,640]{2,1,0:T(8,128)(2,1)S(1)}, u32[]{:S(2)}, u32[]{:S(2)}) async-start(bf16[64,8,640]{2,1,0:T(8,128)(2,1)} %bitcast.12), calls=%async_computation | async-start | bytes 1310720 | tf_op jit(solution)/shard_map/all_to_all | solution.py:269
  15.0 2.3 %collective-permute-start = (bf16[48,2560]{1,0:T(8,128)(2,1)}, bf16[48,2560]{1,0:T(8,128)(2,1)}, u32[]{:S(2)}, u32[]{:S(2)}) collective-permute-start(bf16[48,2560]{1,0:T(8,128)(2,1)} %refs_0_), channel_id=1, source_target_pairs={{0,2},{1,7},{2,4},{3,1},{4,6},{5,3},{6,0},{7,5},{8,10},{9,15},{10,... | collective-permute-start | bytes 737288 | tf_op jit(solution)/shard_map/ppermute | solution.py:262
  17.3 9.6 %collective-permute-done.refs_1_ = bf16[48,2560]{1,0:T(8,128)(2,1)} collective-permute-done((bf16[48,2560]{1,0:T(8,128)(2,1)}, bf16[48,2560]{1,0:T(8,128)(2,1)}, u32[]{:S(2)}, u32[]{:S(2)}) %collective-permute-start) | collective-permute-done | bytes 245792 | tf_op jit(solution)/shard_map/ppermute | solution.py:262
  26.8 1.4 %all-to-all-done = bf16[64,8,640]{2,1,0:T(8,128)(2,1)S(1)} async-done(((bf16[64,8,640]{2,1,0:T(8,128)(2,1)}), bf16[64,8,640]{2,1,0:T(8,128)(2,1)S(1)}, u32[]{:S(2)}, u32[]{:S(2)}) %all-to-all-start) | async-done | bytes 655392 | tf_op jit(solution)/shard_map/all_to_all | solution.py:269
  28.2 2.4 %collective-permute-start.1 = (bf16[512,640]{1,0:T(8,128)(2,1)S(1)}, bf16[512,640]{1,0:T(8,128)(2,1)S(1)}, u32[]{:S(2)}, u32[]{:S(2)}) collective-permute-start(bf16[512,640]{1,0:T(8,128)(2,1)S(1)} %bitcast.6), channel_id=1, source_target_pairs={{0,1},{1,0},{2,3},{3,2},{4,5},{5,4},{6,7},{7,6},{8,9},{9,8},{10,11... | collective-permute-start | bytes 1966088 | tf_op jit(solution)/shard_map/ppermute | solution.py:255
  30.6 0.4 collective-permute-start.2
  31.0 2.3 %collective-permute-start.3 = (bf16[48,2560]{1,0:T(8,128)(2,1)}, bf16[48,2560]{1,0:T(8,128)(2,1)}, u32[]{:S(2)}, u32[]{:S(2)}) collective-permute-start(bf16[48,2560]{1,0:T(8,128)(2,1)} %collective-permute-done.refs_1_), channel_id=1, source_target_pairs={{0,2},{1,7},{2,4},{3,1},{4,6},{5,3},{6,0},{7,5},{8,10},{9,15},{10,... | collective-permute-start | bytes 737288 | tf_op jit(solution)/shard_map/ppermute | solution.py:262
  33.3 3.4 %stage.1 = (bf16[3,2560,256]{2,1,0:T(8,128)(2,1)S(1)}, bf16[3,2560,256]{2,1,0:T(8,128)(2,1)S(1)}) custom-call(bf16[2560,2048]{1,0:T(8,128)(2,1)} %bitcast.8, bf16[2560,2048]{1,0:T(8,128)(2,1)} %bitcast.10), custom_call_target="tpu_custom_call" | custom-call | bytes 10000000 | tf_op jit(solution)/shard_map/stage/pallas_call | solution.py:84
  36.7 0.0 copy-start.2
  36.7 9.1 %routed.1 = bf16[1024,512]{1,0:T(8,128)(2,1)} custom-call(bf16[512,640]{1,0:T(8,128)(2,1)S(1)} %bitcast.7, bf16[512,640]{1,0:T(8,128)(2,1)S(1)} %collective-permute-done.1.other_ref, bf16[2560,2048]{1,0:T(8,128)(2,1)} %bitcast.9, bf16[2560,2048]{1,0:T(8,128)(2,1)} %bitcast.11, bf16[3,2560,256]{2,1,0:T(8,128)(2,1)S(1)} %get-tuple-element.24.gate_first, ...), custom_call_target="tpu_custom_call" | custom-call | flops 5368709120 | bytes 1000000 | tf_op jit(solution)/shard_map/routed/pallas_call | solution.py:159
  45.9 5.6 %all-to-all-start.1 = ((bf16[128,8,512]{2,1,0:T(8,128)(2,1)}), bf16[128,8,512]{2,1,0:T(8,128)(2,1)}, u32[]{:S(2)}, u32[]{:S(2)}) async-start(bf16[128,8,512]{2,1,0:T(8,128)(2,1)} %bitcast.4), calls=%async_computation.1 | async-start | bytes 2097152 | tf_op jit(solution)/shard_map/all_to_all | solution.py:282
  51.5 1.2 %collective-permute-start.4 = (bf16[48,2560]{1,0:T(8,128)(2,1)S(1)}, bf16[48,2560]{1,0:T(8,128)(2,1)S(1)}, u32[]{:S(2)}, u32[]{:S(2)}) collective-permute-start(bf16[48,2560]{1,0:T(8,128)(2,1)S(1)} %copy-done.2), channel_id=1, source_target_pairs={{0,1},{1,0},{2,3},{3,2},{4,5},{5,4},{6,7},{7,6},{8,9},{9,8},{10,11... | collective-permute-start | bytes 737288 | tf_op jit(solution)/shard_map/ppermute | solution.py:255
  52.7 0.1 collective-permute-start.5
  52.8 0.4 collective-permute-start.6
  53.2 0.1 collective-permute-start.7
  53.3 0.5 collective-permute-done.4.refs_4_
  53.8 0.6 collective-permute-done.5.refs_5_
  54.4 0.4 collective-permute-done.6.refs_6_
  54.8 0.4 collective-permute-done.7.refs_7_
  55.1 1.7 %copy-done.1 = bf16[2560,512]{1,0:T(8,128)(2,1)S(1)} copy-done((bf16[2560,512]{1,0:T(8,128)(2,1)S(1)}, bf16[2560,512]{1,0:T(8,128)(2,1)}, u32[]{:S(2)}) %copy-start.1) | copy-done | bytes 2621464
  56.9 4.5 %shared.1 = bf16[384,512]{1,0:T(8,128)(2,1)} custom-call(bf16[48,2560]{1,0:T(8,128)(2,1)S(1)} %copy-done.2, bf16[48,2560]{1,0:T(8,128)(2,1)} %collective-permute-done.refs_1_, bf16[48,2560]{1,0:T(8,128)(2,1)} %collective-permute-done.2.refs_2_, bf16[48,2560]{1,0:T(8,128)(2,1)} %collective-permute-done.3.refs_3_, ...), custom_call_target="tpu_custom_call" | custom-call | flops 2013265920 | bytes 8000000 | tf_op jit(solution)/shard_map/shared/pallas_call | solution.py:205
  61.4 8.7 %all-to-all-done.1 = bf16[128,8,512]{2,1,0:T(8,128)(2,1)} async-done(((bf16[128,8,512]{2,1,0:T(8,128)(2,1)}), bf16[128,8,512]{2,1,0:T(8,128)(2,1)}, u32[]{:S(2)}, u32[]{:S(2)}) %all-to-all-start.1) | async-done | bytes 1048608 | tf_op jit(solution)/shard_map/all_to_all | solution.py:282
  70.0 2.7 %collect.1 = bf16[48,4096]{1,0:T(8,128)(2,1)} custom-call(bf16[1024,512]{1,0:T(8,128)(2,1)} %bitcast.5.back_ref, s32[48]{0:T(128)S(1)} %copy-done.3), custom_call_target="tpu_custom_call" | custom-call | flops 400000000 | bytes 1500000 | tf_op jit(solution)/shard_map/collect/pallas_call | solution.py:245
  (9 shorter events, 0.0 us)
Async XLA Ops:
  3.0 25.2 %all-to-all-start = ((bf16[64,8,640]{2,1,0:T(8,128)(2,1)}), bf16[64,8,640]{2,1,0:T(8,128)(2,1)S(1)}, u32[]{:S(2)}, u32[]{:S(2)}) async-start(bf16[64,8,640]{2,1,0:T(8,128)(2,1)} %bitcast.12), calls=%async_computation | async-start | bytes 1310720 | tf_op jit(solution)/shard_map/all_to_all | solution.py:269
  15.0 11.9 %collective-permute-start = (bf16[48,2560]{1,0:T(8,128)(2,1)}, bf16[48,2560]{1,0:T(8,128)(2,1)}, u32[]{:S(2)}, u32[]{:S(2)}) collective-permute-start(bf16[48,2560]{1,0:T(8,128)(2,1)} %refs_0_), channel_id=1, source_target_pairs={{0,2},{1,7},{2,4},{3,1},{4,6},{5,3},{6,0},{7,5},{8,10},{9,15},{10,... | collective-permute-start | bytes 737288 | tf_op jit(solution)/shard_map/ppermute | solution.py:262
  28.2 8.5 %collective-permute-start.1 = (bf16[512,640]{1,0:T(8,128)(2,1)S(1)}, bf16[512,640]{1,0:T(8,128)(2,1)S(1)}, u32[]{:S(2)}, u32[]{:S(2)}) collective-permute-start(bf16[512,640]{1,0:T(8,128)(2,1)S(1)} %bitcast.6), channel_id=1, source_target_pairs={{0,1},{1,0},{2,3},{3,2},{4,5},{5,4},{6,7},{7,6},{8,9},{9,8},{10,11... | collective-permute-start | bytes 1966088 | tf_op jit(solution)/shard_map/ppermute | solution.py:255
  30.6 15.2 %collective-permute-start.2 = (bf16[48,2560]{1,0:T(8,128)(2,1)}, bf16[48,2560]{1,0:T(8,128)(2,1)}, u32[]{:S(2)}, u32[]{:S(2)}) collective-permute-start(bf16[48,2560]{1,0:T(8,128)(2,1)} %refs_0_), channel_id=1, source_target_pairs={{0,6},{1,3},{2,0},{3,5},{4,2},{5,7},{6,4},{7,1},{8,14},{9,11},{10,... | collective-permute-start | bytes 737288 | tf_op jit(solution)/shard_map/ppermute | solution.py:262
  31.0 14.9 %collective-permute-start.3 = (bf16[48,2560]{1,0:T(8,128)(2,1)}, bf16[48,2560]{1,0:T(8,128)(2,1)}, u32[]{:S(2)}, u32[]{:S(2)}) collective-permute-start(bf16[48,2560]{1,0:T(8,128)(2,1)} %collective-permute-done.refs_1_), channel_id=1, source_target_pairs={{0,2},{1,7},{2,4},{3,1},{4,6},{5,3},{6,0},{7,5},{8,10},{9,15},{10,... | collective-permute-start | bytes 737288 | tf_op jit(solution)/shard_map/ppermute | solution.py:262
  36.7 14.8 %copy-start.2 = (bf16[48,2560]{1,0:T(8,128)(2,1)S(1)}, bf16[48,2560]{1,0:T(8,128)(2,1)}, u32[]{:S(2)}) copy-start(bf16[48,2560]{1,0:T(8,128)(2,1)} %refs_0_) | copy-start | bytes 737284
  36.7 18.4 %copy-start = (bf16[2560,512]{1,0:T(8,128)(2,1)S(1)}, bf16[2560,512]{1,0:T(8,128)(2,1)}, u32[]{:S(2)}) copy-start(bf16[2560,512]{1,0:T(8,128)(2,1)} %refs_8_.1) | copy-start | bytes 7864324
  45.9 24.2 %copy-start.3 = (s32[48]{0:T(128)S(1)}, s32[48]{0:T(128)}, u32[]{:S(2)}) copy-start(s32[48]{0:T(128)} %ids_ref.3) | copy-start | bytes 580
  45.9 24.1 %all-to-all-start.1 = ((bf16[128,8,512]{2,1,0:T(8,128)(2,1)}), bf16[128,8,512]{2,1,0:T(8,128)(2,1)}, u32[]{:S(2)}, u32[]{:S(2)}) async-start(bf16[128,8,512]{2,1,0:T(8,128)(2,1)} %bitcast.4), calls=%async_computation.1 | async-start | bytes 2097152 | tf_op jit(solution)/shard_map/all_to_all | solution.py:282
  51.5 2.4 %collective-permute-start.4 = (bf16[48,2560]{1,0:T(8,128)(2,1)S(1)}, bf16[48,2560]{1,0:T(8,128)(2,1)S(1)}, u32[]{:S(2)}, u32[]{:S(2)}) collective-permute-start(bf16[48,2560]{1,0:T(8,128)(2,1)S(1)} %copy-done.2), channel_id=1, source_target_pairs={{0,1},{1,0},{2,3},{3,2},{4,5},{5,4},{6,7},{7,6},{8,9},{9,8},{10,11... | collective-permute-start | bytes 737288 | tf_op jit(solution)/shard_map/ppermute | solution.py:255
  52.7 1.7 %collective-permute-start.5 = (bf16[48,2560]{1,0:T(8,128)(2,1)}, bf16[48,2560]{1,0:T(8,128)(2,1)S(1)}, u32[]{:S(2)}, u32[]{:S(2)}) collective-permute-start(bf16[48,2560]{1,0:T(8,128)(2,1)} %collective-permute-done.refs_1_), channel_id=1, source_target_pairs={{0,1},{1,0},{2,3},{3,2},{4,5},{5,4},{6,7},{7,6},{8,9},{9,8},{10,11... | collective-permute-start | bytes 737288 | tf_op jit(solution)/shard_map/ppermute | solution.py:255
  52.8 2.0 %collective-permute-start.6 = (bf16[48,2560]{1,0:T(8,128)(2,1)}, bf16[48,2560]{1,0:T(8,128)(2,1)S(1)}, u32[]{:S(2)}, u32[]{:S(2)}) collective-permute-start(bf16[48,2560]{1,0:T(8,128)(2,1)} %collective-permute-done.2.refs_2_), channel_id=1, source_target_pairs={{0,1},{1,0},{2,3},{3,2},{4,5},{5,4},{6,7},{7,6},{8,9},{9,8},{10,11... | collective-permute-start | bytes 737288 | tf_op jit(solution)/shard_map/ppermute | solution.py:255
  53.2 1.9 %collective-permute-start.7 = (bf16[48,2560]{1,0:T(8,128)(2,1)}, bf16[48,2560]{1,0:T(8,128)(2,1)S(1)}, u32[]{:S(2)}, u32[]{:S(2)}) collective-permute-start(bf16[48,2560]{1,0:T(8,128)(2,1)} %collective-permute-done.3.refs_3_), channel_id=1, source_target_pairs={{0,1},{1,0},{2,3},{3,2},{4,5},{5,4},{6,7},{7,6},{8,9},{9,8},{10,11... | collective-permute-start | bytes 737288 | tf_op jit(solution)/shard_map/ppermute | solution.py:255
  55.1 1.7 %copy-start.1 = (bf16[2560,512]{1,0:T(8,128)(2,1)S(1)}, bf16[2560,512]{1,0:T(8,128)(2,1)}, u32[]{:S(2)}) copy-start(bf16[2560,512]{1,0:T(8,128)(2,1)} %refs_9_.1) | copy-start | bytes 7864324

commit v2 on v1

v2 whole, which is shorter than its diff:
```python
import jax
import jax.numpy as jnp
from jax import lax
from jax.experimental import pallas as pl
from jax.experimental.pallas import tpu as pltpu
from jax.sharding import Mesh, PartitionSpec as P

CAP = 2
LANES = 128
TILE = 256
F32 = jnp.float32
BF16 = jnp.bfloat16
I32 = jnp.int32


def iota(shape, dim):
    return lax.broadcasted_iota(I32, shape, dim)


def column(row, n):
    eye = iota((n, n), 0) == iota((n, n), 1)
    return jnp.sum(jnp.where(eye, jnp.broadcast_to(row, (n, n)), 0), axis=1, keepdims=True)


def dispatch_kernel(tokens_ref, scores_ref, ids_ref, send_ref):
    n, width = tokens_ref.shape
    pieces = 8 // CAP
    part = width // pieces
    ids_row = ids_ref[...].reshape(1, n)
    ids_col = column(ids_row, n)
    score_col = column(scores_ref[...].reshape(1, n), n)
    tokens = tokens_ref[...]
    scaled = (tokens.astype(F32) * score_col).astype(BF16)
    earlier = (ids_col == ids_row) & (iota((n, n), 0) < iota((n, n), 1))
    rank_row = jnp.sum(earlier.astype(I32), axis=0, keepdims=True)
    entry = 8 * ids_row + pieces * rank_row
    rows = iota((send_ref.shape[0], n), 0)
    hot = jnp.concatenate(
        [(rows == entry + j).astype(F32).astype(BF16) for j in range(pieces)], axis=1
    )
    stack = jnp.concatenate([scaled[:, j * part : (j + 1) * part] for j in range(pieces)], axis=0)
    send_ref[...] = jnp.dot(hot, stack, preferred_element_type=F32).astype(BF16)


def dispatch(tokens, scores, expert_ids, chips):
    n, width = tokens.shape
    return pl.pallas_call(
        dispatch_kernel,
        out_shape=jax.ShapeDtypeStruct((chips * 8, width * CAP // 8), BF16),
        compiler_params=pltpu.CompilerParams(vmem_limit_bytes=8 << 20),
        name="dispatch",
        cost_estimate=pl.CostEstimate(flops=2 * 10**10, bytes_accessed=2 * 10**6, transcendentals=0),
    )(
        tokens,
        pltpu.with_memory_space_constraint(scores, pltpu.HBM),
        pltpu.with_memory_space_constraint(expert_ids, pltpu.HBM),
    )


def silu_mul(gate, up):
    return gate / (1.0 + jnp.exp(-gate)) * up


def routed_rows(rows_ref, hidden_ref, moved, gate_ref, up_ref, emit):
    chips = moved.shape[0] // 8
    part = moved.shape[1]
    pieces = 8 // CAP
    to = iota((8 * chips, 8 * chips), 0)
    at = 8 * (to % chips) + pieces * (to // chips % CAP) + to // (CAP * chips)
    perm = (iota((8 * chips, 8 * chips), 1) == at).astype(F32).astype(BF16)
    moved = jnp.dot(perm, moved, preferred_element_type=F32).astype(BF16)
    for j in range(pieces):
        rows_ref[:, j * part : (j + 1) * part] = moved[
            j * CAP * chips : (j + 1) * CAP * chips
        ]
    units = gate_ref.shape[1] // pieces
    for q in range(units // TILE):
        for j in range(pieces):
            lane = j * units + q * TILE
            gate_tile = gate_ref[:, lane : lane + TILE]
            up_tile = up_ref[:, lane : lane + TILE]
            gate = jnp.dot(rows_ref[...], gate_tile, preferred_element_type=F32)
            up = jnp.dot(rows_ref[...], up_tile, preferred_element_type=F32)
            hidden = silu_mul(gate, up)
            for s in range(CAP):
                for k in range(TILE // LANES):
                    hidden_ref[k, pl.ds(pieces * s + j, chips, stride=8), :] = hidden[
                        s * chips : (s + 1) * chips, k * LANES : (k + 1) * LANES
                    ]
        for k in range(TILE // LANES):
            emit(q, k, hidden_ref[k].reshape(chips, 8, LANES).astype(BF16))


def routed_own_kernel(own_ref, gate_ref, up_ref, out_ref, rows_ref, hidden_ref):
    def emit(q, k, block):
        lane = q * TILE + k * LANES
        out_ref[:, :, lane : lane + LANES] = block

    routed_rows(rows_ref, hidden_ref, own_ref[...], gate_ref, up_ref, emit)


def routed_other_kernel(
    other_ref, mine_ref, gate_ref, up_ref, out_ref, rows_ref, hidden_ref, block_ref, sems
):
    core = lax.axis_index("core")
    splits = block_ref.shape[2] // TILE
    first = pltpu.make_async_copy(mine_ref, out_ref.at[:, core], sems.at[splits])
    first.start()
    copies = []

    def emit(q, k, block):
        lane = q * TILE + k * LANES
        block_ref[:, :, lane : lane + LANES] = block
        if k == TILE // LANES - 1:
            lanes = slice(q * TILE, (q + 1) * TILE)
            copies.append(
                pltpu.make_async_copy(
                    block_ref.at[:, :, lanes], out_ref.at[:, 1 - core, :, lanes], sems.at[q]
                )
            )
            copies[-1].start()

    routed_rows(rows_ref, hidden_ref, other_ref[...], gate_ref, up_ref, emit)
    first.wait()
    for copy in copies:
        copy.wait()


def routed_estimate(rows, width, units):
    return pl.CostEstimate(flops=4 * rows * width * units, bytes_accessed=10**6, transcendentals=0)


def routed(own, other, gate, up):
    rows, part = own.shape
    width, units = gate.shape
    pieces = 8 // CAP
    chips = rows // 8
    vmem = pl.BlockSpec(memory_space=pltpu.VMEM)
    hbm = pl.BlockSpec(memory_space=pltpu.HBM)
    work = [
        pltpu.VMEM((CAP * chips, width), BF16),
        pltpu.VMEM((TILE // LANES, 8 * chips, LANES), F32),
    ]
    block = (chips, 8, units // pieces)
    mine = pl.pallas_call(
        routed_own_kernel,
        out_shape=pltpu.VMEM(block, BF16),
        in_specs=[vmem] * 3,
        out_specs=vmem,
        scratch_shapes=work,
        compiler_params=pltpu.CompilerParams(vmem_limit_bytes=12 << 20),
        name="routed_own",
        cost_estimate=routed_estimate(CAP * chips, width, units),
    )(own, gate, up)
    return pl.pallas_call(
        routed_other_kernel,
        out_shape=jax.ShapeDtypeStruct((chips, 2) + block[1:], BF16),
        in_specs=[vmem] * 4,
        out_specs=hbm,
        scratch_shapes=work
        + [pltpu.VMEM(block, BF16), pltpu.SemaphoreType.DMA((units // pieces // TILE + 1,))],
        compiler_params=pltpu.CompilerParams(vmem_limit_bytes=12 << 20),
        name="routed_other",
        cost_estimate=routed_estimate(CAP * chips, width, units),
    )(other, mine, gate, up)


def shared_kernel(*refs):
    gate_ref, up_ref, out_ref = refs[-3:]
    blocks = refs[:-3]
    core = lax.axis_index("core")
    y = lax.axis_index("y")
    ring = len(blocks) // 2
    n = blocks[0].shape[0]
    for c in range(2):
        rows = jnp.concatenate([ref[...] for ref in blocks[ring * c : ring * (c + 1)]], axis=0)
        gate = jnp.dot(rows, gate_ref[...], preferred_element_type=F32)
        up = jnp.dot(rows, up_ref[...], preferred_element_type=F32)
        hidden = silu_mul(gate, up).astype(BF16)
        core_of = core if c == 0 else 1 - core
        step = 1 - 2 * core_of
        for i, back in enumerate((0, 1, -1, 2)):
            from_y = lax.rem(y - back * step + 2 * ring, ring)
            at = pl.multiple_of(n * (2 * from_y + core_of), 16)
            out_ref[pl.ds(at, n), :] = hidden[n * i : n * (i + 1)]


def shared(blocks, shared_gate, shared_up):
    n, width = blocks[0].shape
    units = shared_gate.shape[1]
    tile = 256
    whole = pl.BlockSpec((n, width), lambda q: (0, 0))
    weight = pl.BlockSpec((width, tile), lambda q: (0, q))
    return pl.pallas_call(
        shared_kernel,
        out_shape=jax.ShapeDtypeStruct((len(blocks) * n, units), BF16),
        grid=(units // tile,),
        in_specs=[whole] * len(blocks) + [weight, weight],
        out_specs=pl.BlockSpec((len(blocks) * n, tile), lambda q: (0, q)),
        compiler_params=pltpu.CompilerParams(vmem_limit_bytes=32 << 20),
        name="shared",
        cost_estimate=pl.CostEstimate(
            flops=7 * 10**9, bytes_accessed=8 * 10**6, transcendentals=0
        ),
    )(*blocks, shared_gate, shared_up)


def collect_kernel(back_ref, ids_ref, out_ref):
    n = out_ref.shape[0]
    pieces = 8 // CAP
    part = back_ref.shape[1]
    ids_row = ids_ref[...].reshape(1, n)
    ids_col = column(ids_row, n)
    earlier = (ids_col == ids_row) & (iota((n, n), 1) < iota((n, n), 0))
    rank_col = jnp.sum(earlier.astype(I32), axis=1, keepdims=True)
    entry = 16 * ids_col + pieces * rank_col
    cells = iota((n, back_ref.shape[0]), 1)
    hot = jnp.concatenate(
        [
            (cells == entry + (8 * h + j)).astype(F32).astype(BF16)
            for h in range(2)
            for j in range(pieces)
        ],
        axis=0,
    )
    picked = jnp.dot(hot, back_ref[...], preferred_element_type=F32).astype(BF16)
    for q in range(2 * pieces):
        out_ref[:, q * part : (q + 1) * part] = picked[q * n : (q + 1) * n]


def collect(back, expert_ids):
    rows, part = back.shape
    n = expert_ids.shape[0]
    return pl.pallas_call(
        collect_kernel,
        out_shape=jax.ShapeDtypeStruct((n, 8 * part), BF16),
        compiler_params=pltpu.CompilerParams(vmem_limit_bytes=8 << 20),
        name="collect",
        cost_estimate=pl.CostEstimate(flops=4 * 10**8, bytes_accessed=15 * 10**5, transcendentals=0),
    )(back, expert_ids)


def swap(x):
    return lax.ppermute(x, "core", [(0, 1), (1, 0)])


def turn(x, ring, step):
    pairs = [
        (2 * y + c, 2 * ((y + step * (1 - 2 * c)) % ring) + c) for y in range(ring) for c in range(2)
    ]
    return lax.ppermute(x, ("y", "core"), pairs)


def shards(tokens, scores, expert_ids, gate_halves, up_halves, shared_gate, shared_up):
    ring = lax.axis_size("y")
    chips = lax.axis_size("wide") * ring
    send = dispatch(tokens, scores, expert_ids, chips)
    arrived = lax.all_to_all(
        send.reshape(chips, 8, send.shape[1]), ("wide", "y"), split_axis=0, concat_axis=0, tiled=True
    ).reshape(send.shape)
    gate = pltpu.with_memory_space_constraint(gate_halves[0], pltpu.VMEM)
    up = pltpu.with_memory_space_constraint(up_halves[0], pltpu.VMEM)
    arrived, mine = lax.optimization_barrier((arrived, tokens))
    arrived_other = swap(arrived)
    after = turn(mine, ring, 1)
    before = turn(mine, ring, -1)
    opposite = turn(mine, ring, 2)
    hidden = routed(arrived, arrived_other, gate, up)
    back = lax.all_to_all(
        hidden.reshape(2 * chips, 8, hidden.shape[3]),
        ("wide", "y", "core"),
        split_axis=0,
        concat_axis=0,
        tiled=True,
    ).reshape(16 * chips, hidden.shape[3])
    blocks = [tokens, after, before, opposite]
    blocks = blocks + [swap(block) for block in blocks]
    blocks = lax.optimization_barrier((*blocks, hidden))[:-1]
    shared_hidden = shared(blocks, shared_gate, shared_up)
    back, shared_hidden = lax.optimization_barrier((back, shared_hidden))
    return collect(back, expert_ids), shared_hidden


def solution(mesh):
    wide, narrow = mesh.devices.shape
    fine = Mesh(mesh.devices.reshape(wide, narrow // 2, 2), ("wide", "y", "core"))
    every = ("wide", "y", "core")
    placed = (
        P(every, None),
        P(every),
        P(every),
        P(every, None, None),
        P(every, None, None),
        P(None, ("y", "core")),
        P(None, ("y", "core")),
    )
    return jax.shard_map(
        shards,
        mesh=fine,
        in_specs=placed,
        out_specs=(P(every, None), P("wide", ("y", "core"))),
        check_vma=False,
    )
```

time: 73.1 us -> 67.5 us (0.923)
  blocking collectives: 0 us -> 25.2 us
  starting transfers between devices: 26.7 us -> 13 us
  waiting for transfers between devices: 21.4 us -> 9.41 us
  Pallas kernels: 22.1 us -> 15.4 us
  local copies, waits for them, and re-layouts: 1.76 us -> 3.49 us
    all_to_all x0 -> x1, blocking collectives: none -> 25.2 us  [shards(): lax.all_to_all(send.reshape(chips, 8, send.shape[1]), ('wide', 'y'), spli...]
    all_to_all x2 -> x1, starting transfers between devices: 17.6 us -> 6.67 us  [shards(): lax.all_to_all(hidden.reshape(2 * chips, 8, hidden.shape[3]), ('wide', 'y...]
    ppermute x3, waiting for transfers between devices: 9.58 us -> 0.01 us  [turn(): return lax.ppermute(x, ('y', 'core'), pairs)]
    pallas_call x2, Pallas kernels: 12.5 us -> 8.03 us  [the longest x1 4.43 us: routed(): pl.pallas_call(routed_other_kernel, out_shape=jax.ShapeDtypeStruct((chips...]
    ppermute x3, starting transfers between devices: 4.97 us -> 2.19 us  [turn(): return lax.ppermute(x, ('y', 'core'), pairs)]
    all_to_all x2 -> x1, waiting for transfers between devices: 10 us -> 7.8 us  [shards(): lax.all_to_all(hidden.reshape(2 * chips, 8, hidden.shape[3]), ('wide', 'y...]
    unnamed x8 -> x10, local copies, waits for them, and re-layouts: 1.76 us -> 3.49 us
    pallas_call x1, Pallas kernels: 2.68 us -> 1.46 us  [collect(): pl.pallas_call(collect_kernel, out_shape=jax.ShapeDtypeStruct((n, 8 * par...]
  transfers between devices with their start and end apart: 10 -> 9, of which waited for: 7 -> 5; matrix products, arithmetic and copies ran while one was open for 0% -> 0% of each run, Pallas kernels for 23% -> 18%
where the time goes in v2:
time: 67.5 us; the launch traced here: 67.2 us
  blocking collectives  25.2 us (37%)
  Pallas kernels  15.4 us (23%)
  starting transfers between devices  13 us (19%)
  waiting for transfers between devices  9.41 us (14%)
  local copies, waits for them, and re-layouts  3.49 us (5%)
  between operations  0.7 us (1%)
    all_to_all x1, blocking collectives, shards(): lax.all_to_all(send.reshape(chips, 8, send.shape[1]), ('wide', 'y'), spli...  25.2 us
    all_to_all x1, waiting for transfers between devices, shards(): lax.all_to_all(hidden.reshape(2 * chips, 8, hidden.shape[3]), ('wide', 'y...  7.8 us
    all_to_all x1, starting transfers between devices, shards(): lax.all_to_all(hidden.reshape(2 * chips, 8, hidden.shape[3]), ('wide', 'y...  6.67 us
    pallas_call x1, Pallas kernels, routed(): pl.pallas_call(routed_other_kernel, out_shape=jax.ShapeDtypeStruct((chips...  4.43 us
    pallas_call x1, Pallas kernels, shared(): pl.pallas_call(shared_kernel, out_shape=jax.ShapeDtypeStruct((len(blocks)...  4.25 us
    ppermute x5, starting transfers between devices, swap(): return lax.ppermute(x, 'core', [(0, 1), (1, 0)])  4.13 us
    pallas_call x1, Pallas kernels, routed(): pl.pallas_call(routed_own_kernel, out_shape=pltpu.VMEM(block, BF16), in_s...  3.59 us
    unnamed x10, local copies, waits for them, and re-layouts  3.49 us
  transfers between devices with their start and end apart: 9, of which 5 were waited for; matrix products, arithmetic and copies ran while one was open for 0% of the time, Pallas kernels for 18%

profile of v2, /device:TPU:1, one launch (start us, length us, event | category | flops | bytes accessed | tf_op | source)
XLA Modules:
  0.0 67.2 jit_solution(3656498547924863156)
XLA Ops:
  0.7 1.7 %dispatch.1 = bf16[512,640]{1,0:T(8,128)(2,1)S(1)} custom-call(bf16[48,2560]{1,0:T(8,128)(2,1)} %refs_0_, f32[48]{0:T(128)} %scores_ref.1, s32[48]{0:T(128)} %ids_ref.3), custom_call_target="tpu_custom_call" | custom-call | flops 20000000000 | bytes 2000000 | tf_op jit(solution)/shard_map/dispatch/pallas_call | solution.py:47
  2.3 25.2 %all_to_all.10 = bf16[64,8,640]{2,1,0:T(8,128)(2,1)S(1)} all-to-all(bf16[64,8,640]{2,1,0:T(8,128)(2,1)S(1)} %bitcast.13), channel_id=1, replica_groups=mesh['wide'=16,'y'=4,'core'=2] {'wide','y'}, dimensions={0} | all-to-all | bytes 1310720 | tf_op jit(solution)/shard_map/all_to_all | solution.py:258
  27.6 2.4 %collective-permute-start = (bf16[512,640]{1,0:T(8,128)(2,1)S(1)}, bf16[512,640]{1,0:T(8,128)(2,1)S(1)}, u32[]{:S(2)}, u32[]{:S(2)}) collective-permute-start(bf16[512,640]{1,0:T(8,128)(2,1)S(1)} %bitcast.10), channel_id=1, source_target_pairs={{0,1},{1,0},{2,3},{3,2},{4,5},{5,4},{6,7},{7,6},{8,9},{9,8},{10,11... | collective-permute-start | bytes 1966088 | tf_op jit(solution)/shard_map/ppermute | solution.py:244
  29.9 0.3 collective-permute-start.1
  30.2 1.2 %collective-permute-start.2 = (bf16[48,2560]{1,0:T(8,128)(2,1)}, bf16[48,2560]{1,0:T(8,128)(2,1)S(1)}, u32[]{:S(2)}, u32[]{:S(2)}) collective-permute-start(bf16[48,2560]{1,0:T(8,128)(2,1)} %refs_0_), channel_id=1, source_target_pairs={{0,6},{1,3},{2,0},{3,5},{4,2},{5,7},{6,4},{7,1},{8,14},{9,11},{10,... | collective-permute-start | bytes 737288 | tf_op jit(solution)/shard_map/ppermute | solution.py:251
  31.4 0.7 %collective-permute-start.3 = (bf16[48,2560]{1,0:T(8,128)(2,1)}, bf16[48,2560]{1,0:T(8,128)(2,1)S(1)}, u32[]{:S(2)}, u32[]{:S(2)}) collective-permute-start(bf16[48,2560]{1,0:T(8,128)(2,1)} %refs_0_), channel_id=1, source_target_pairs={{0,4},{1,5},{2,6},{3,7},{4,0},{5,1},{6,2},{7,3},{8,12},{9,13},{10,... | collective-permute-start | bytes 737288 | tf_op jit(solution)/shard_map/ppermute | solution.py:251
  32.1 3.6 %routed_own.1.mine_ref = bf16[64,8,512]{2,1,0:T(8,128)(2,1)S(1)} custom-call(bf16[512,640]{1,0:T(8,128)(2,1)S(1)} %bitcast.11, bf16[2560,2048]{1,0:T(8,128)(2,1)S(1)} %bitcast.6, bf16[2560,2048]{1,0:T(8,128)(2,1)S(1)} %bitcast.8), custom_call_target="tpu_custom_call" | custom-call | flops 2684354560 | bytes 1000000 | tf_op jit(solution)/shard_map/routed_own/pallas_call | solution.py:145
  35.7 0.0 collective-permute-done.other_ref
  35.7 4.4 %routed_other.1 = bf16[64,2,8,512]{3,2,1,0:T(8,128)(2,1)} custom-call(bf16[512,640]{1,0:T(8,128)(2,1)S(1)} %collective-permute-done.other_ref, bf16[64,8,512]{2,1,0:T(8,128)(2,1)S(1)} %routed_own.1.mine_ref, bf16[2560,2048]{1,0:T(8,128)(2,1)S(1)} %bitcast.7, bf16[2560,2048]{1,0:T(8,128)(2,1)S(1)} %bitcast.9), custom_call_target="tpu_custom_call" | custom-call | flops 2684354560 | bytes 1000000 | tf_op jit(solution)/shard_map/routed_other/pallas_call | solution.py:155
  40.2 0.0 copy-start.4
  40.2 6.7 %all-to-all-start.1 = ((bf16[128,8,512]{2,1,0:T(8,128)(2,1)}), bf16[128,8,512]{2,1,0:T(8,128)(2,1)S(1)}, u32[]{:S(2)}, u32[]{:S(2)}) async-start(bf16[128,8,512]{2,1,0:T(8,128)(2,1)} %bitcast.4), calls=%async_computation.1 | async-start | bytes 2097152 | tf_op jit(solution)/shard_map/all_to_all | solution.py:269
  46.9 1.1 %collective-permute-start.4 = (bf16[48,2560]{1,0:T(8,128)(2,1)}, bf16[48,2560]{1,0:T(8,128)(2,1)S(1)}, u32[]{:S(2)}, u32[]{:S(2)}) collective-permute-start(bf16[48,2560]{1,0:T(8,128)(2,1)} %refs_0_), channel_id=1, source_target_pairs={{0,1},{1,0},{2,3},{3,2},{4,5},{5,4},{6,7},{7,6},{8,9},{9,8},{10,11... | collective-permute-start | bytes 737288 | tf_op jit(solution)/shard_map/ppermute | solution.py:244
  48.0 0.1 collective-permute-start.5
  48.1 0.4 collective-permute-start.6
  48.6 0.1 collective-permute-start.7
  48.7 0.7 %collective-permute-done.4.refs_4_ = bf16[48,2560]{1,0:T(8,128)(2,1)S(1)} collective-permute-done((bf16[48,2560]{1,0:T(8,128)(2,1)}, bf16[48,2560]{1,0:T(8,128)(2,1)S(1)}, u32[]{:S(2)}, u32[]{:S(2)}) %collective-permute-start.4) | collective-permute-done | bytes 245792 | tf_op jit(solution)/shard_map/ppermute | solution.py:244
  49.4 0.2 collective-permute-done.5.refs_5_
  49.5 0.4 collective-permute-done.6.refs_6_
  49.9 0.4 collective-permute-done.7.refs_7_
  50.3 1.7 %copy-done.2 = bf16[2560,512]{1,0:T(8,128)(2,1)S(1)} copy-done((bf16[2560,512]{1,0:T(8,128)(2,1)S(1)}, bf16[2560,512]{1,0:T(8,128)(2,1)}, u32[]{:S(2)}) %copy-start.2) | copy-done | bytes 2621464
  52.0 1.7 %copy-done.3 = bf16[2560,512]{1,0:T(8,128)(2,1)S(1)} copy-done((bf16[2560,512]{1,0:T(8,128)(2,1)S(1)}, bf16[2560,512]{1,0:T(8,128)(2,1)}, u32[]{:S(2)}) %copy-start.3) | copy-done | bytes 2621464
  53.7 4.3 %shared.1 = bf16[384,512]{1,0:T(8,128)(2,1)} custom-call(bf16[48,2560]{1,0:T(8,128)(2,1)} %refs_0_, bf16[48,2560]{1,0:T(8,128)(2,1)S(1)} %collective-permute-done.1.refs_1_, bf16[48,2560]{1,0:T(8,128)(2,1)S(1)} %collective-permute-done.2.refs_2_, bf16[48,2560]{1,0:T(8,128)(2,1)S(1)} %collective-permute-done.3.refs_3_, ...), custom_call_target="tpu_custom_call" | custom-call | flops 7000000000 | bytes 8000000 | tf_op jit(solution)/shard_map/shared/pallas_call | solution.py:194
  58.0 7.8 %all-to-all-done.1 = bf16[128,8,512]{2,1,0:T(8,128)(2,1)S(1)} async-done(((bf16[128,8,512]{2,1,0:T(8,128)(2,1)}), bf16[128,8,512]{2,1,0:T(8,128)(2,1)S(1)}, u32[]{:S(2)}, u32[]{:S(2)}) %all-to-all-start.1) | async-done | bytes 1048608 | tf_op jit(solution)/shard_map/all_to_all | solution.py:269
  65.8 1.5 %collect.1 = bf16[48,4096]{1,0:T(8,128)(2,1)} custom-call(bf16[1024,512]{1,0:T(8,128)(2,1)S(1)} %bitcast.12, s32[48]{0:T(128)S(1)} %copy-done.4), custom_call_target="tpu_custom_call" | custom-call | flops 400000000 | bytes 1500000 | tf_op jit(solution)/shard_map/collect/pallas_call | solution.py:234
  (10 shorter events, 0.0 us)
Async XLA Ops:
  0.6 31.5 %copy-start = (bf16[1,2560,2048]{2,1,0:T(8,128)(2,1)S(1)}, bf16[1,2560,2048]{2,1,0:T(8,128)(2,1)}, u32[]{:S(2)}) copy-start(bf16[1,2560,2048]{2,1,0:T(8,128)(2,1)} %param.10) | copy-start | bytes 31457284
  0.6 31.5 %copy-start.1 = (bf16[1,2560,2048]{2,1,0:T(8,128)(2,1)S(1)}, bf16[1,2560,2048]{2,1,0:T(8,128)(2,1)}, u32[]{:S(2)}) copy-start(bf16[1,2560,2048]{2,1,0:T(8,128)(2,1)} %param.11) | copy-start | bytes 31457284
  27.6 8.2 %collective-permute-start = (bf16[512,640]{1,0:T(8,128)(2,1)S(1)}, bf16[512,640]{1,0:T(8,128)(2,1)S(1)}, u32[]{:S(2)}, u32[]{:S(2)}) collective-permute-start(bf16[512,640]{1,0:T(8,128)(2,1)S(1)} %bitcast.10), channel_id=1, source_target_pairs={{0,1},{1,0},{2,3},{3,2},{4,5},{5,4},{6,7},{7,6},{8,9},{9,8},{10,11... | collective-permute-start | bytes 1966088 | tf_op jit(solution)/shard_map/ppermute | solution.py:244
  29.9 18.1 %collective-permute-start.1 = (bf16[48,2560]{1,0:T(8,128)(2,1)}, bf16[48,2560]{1,0:T(8,128)(2,1)S(1)}, u32[]{:S(2)}, u32[]{:S(2)}) collective-permute-start(bf16[48,2560]{1,0:T(8,128)(2,1)} %refs_0_), channel_id=1, source_target_pairs={{0,2},{1,7},{2,4},{3,1},{4,6},{5,3},{6,0},{7,5},{8,10},{9,15},{10,... | collective-permute-start | bytes 737288 | tf_op jit(solution)/shard_map/ppermute | solution.py:251
  30.2 17.9 %collective-permute-start.2 = (bf16[48,2560]{1,0:T(8,128)(2,1)}, bf16[48,2560]{1,0:T(8,128)(2,1)S(1)}, u32[]{:S(2)}, u32[]{:S(2)}) collective-permute-start(bf16[48,2560]{1,0:T(8,128)(2,1)} %refs_0_), channel_id=1, source_target_pairs={{0,6},{1,3},{2,0},{3,5},{4,2},{5,7},{6,4},{7,1},{8,14},{9,11},{10,... | collective-permute-start | bytes 737288 | tf_op jit(solution)/shard_map/ppermute | solution.py:251
  31.4 17.1 %collective-permute-start.3 = (bf16[48,2560]{1,0:T(8,128)(2,1)}, bf16[48,2560]{1,0:T(8,128)(2,1)S(1)}, u32[]{:S(2)}, u32[]{:S(2)}) collective-permute-start(bf16[48,2560]{1,0:T(8,128)(2,1)} %refs_0_), channel_id=1, source_target_pairs={{0,4},{1,5},{2,6},{3,7},{4,0},{5,1},{6,2},{7,3},{8,12},{9,13},{10,... | collective-permute-start | bytes 737288 | tf_op jit(solution)/shard_map/ppermute | solution.py:251
  40.2 25.6 %copy-start.4 = (s32[48]{0:T(128)S(1)}, s32[48]{0:T(128)}, u32[]{:S(2)}) copy-start(s32[48]{0:T(128)} %ids_ref.3) | copy-start | bytes 580
  40.2 25.6 %all-to-all-start.1 = ((bf16[128,8,512]{2,1,0:T(8,128)(2,1)}), bf16[128,8,512]{2,1,0:T(8,128)(2,1)S(1)}, u32[]{:S(2)}, u32[]{:S(2)}) async-start(bf16[128,8,512]{2,1,0:T(8,128)(2,1)} %bitcast.4), calls=%async_computation.1 | async-start | bytes 2097152 | tf_op jit(solution)/shard_map/all_to_all | solution.py:269
  46.9 2.5 %collective-permute-start.4 = (bf16[48,2560]{1,0:T(8,128)(2,1)}, bf16[48,2560]{1,0:T(8,128)(2,1)S(1)}, u32[]{:S(2)}, u32[]{:S(2)}) collective-permute-start(bf16[48,2560]{1,0:T(8,128)(2,1)} %refs_0_), channel_id=1, source_target_pairs={{0,1},{1,0},{2,3},{3,2},{4,5},{5,4},{6,7},{7,6},{8,9},{9,8},{10,11... | collective-permute-start | bytes 737288 | tf_op jit(solution)/shard_map/ppermute | solution.py:244
  48.0 1.5 %collective-permute-start.5 = (bf16[48,2560]{1,0:T(8,128)(2,1)S(1)}, bf16[48,2560]{1,0:T(8,128)(2,1)S(1)}, u32[]{:S(2)}, u32[]{:S(2)}) collective-permute-start(bf16[48,2560]{1,0:T(8,128)(2,1)S(1)} %collective-permute-done.1.refs_1_), channel_id=1, source_target_pairs={{0,1},{1,0},{2,3},{3,2},{4,5},{5,4},{6,7},{7,6},{8,9},{9,8},{10,11... | collective-permute-start | bytes 737288 | tf_op jit(solution)/shard_map/ppermute | solution.py:244
  48.1 1.8 %collective-permute-start.6 = (bf16[48,2560]{1,0:T(8,128)(2,1)S(1)}, bf16[48,2560]{1,0:T(8,128)(2,1)S(1)}, u32[]{:S(2)}, u32[]{:S(2)}) collective-permute-start(bf16[48,2560]{1,0:T(8,128)(2,1)S(1)} %collective-permute-done.2.refs_2_), channel_id=1, source_target_pairs={{0,1},{1,0},{2,3},{3,2},{4,5},{5,4},{6,7},{7,6},{8,9},{9,8},{10,11... | collective-permute-start | bytes 737288 | tf_op jit(solution)/shard_map/ppermute | solution.py:244
  48.6 1.7 %collective-permute-start.7 = (bf16[48,2560]{1,0:T(8,128)(2,1)S(1)}, bf16[48,2560]{1,0:T(8,128)(2,1)S(1)}, u32[]{:S(2)}, u32[]{:S(2)}) collective-permute-start(bf16[48,2560]{1,0:T(8,128)(2,1)S(1)} %collective-permute-done.3.refs_3_), channel_id=1, source_target_pairs={{0,1},{1,0},{2,3},{3,2},{4,5},{5,4},{6,7},{7,6},{8,9},{9,8},{10,11... | collective-permute-start | bytes 737288 | tf_op jit(solution)/shard_map/ppermute | solution.py:244
  50.2 1.7 %copy-start.2 = (bf16[2560,512]{1,0:T(8,128)(2,1)S(1)}, bf16[2560,512]{1,0:T(8,128)(2,1)}, u32[]{:S(2)}) copy-start(bf16[2560,512]{1,0:T(8,128)(2,1)} %refs_8_.1) | copy-start | bytes 7864324
  52.0 1.7 %copy-start.3 = (bf16[2560,512]{1,0:T(8,128)(2,1)S(1)}, bf16[2560,512]{1,0:T(8,128)(2,1)}, u32[]{:S(2)}) copy-start(bf16[2560,512]{1,0:T(8,128)(2,1)} %refs_9_.1) | copy-start | bytes 7864324

commit v3 on v2

--- a/solution.py
+++ b/solution.py
@@ -51,7 +51,7 @@
         name="dispatch",
         cost_estimate=pl.CostEstimate(flops=2 * 10**10, bytes_accessed=2 * 10**6, transcendentals=0),
     )(
-        tokens,
+        pltpu.with_memory_space_constraint(tokens, pltpu.HBM),
         pltpu.with_memory_space_constraint(scores, pltpu.HBM),
         pltpu.with_memory_space_constraint(expert_ids, pltpu.HBM),
     )
@@ -61,18 +61,25 @@
     return gate / (1.0 + jnp.exp(-gate)) * up
 
 
-def routed_rows(rows_ref, hidden_ref, moved, gate_ref, up_ref, emit):
-    chips = moved.shape[0] // 8
-    part = moved.shape[1]
+def routed_rows(rows_ref, hidden_ref, arrived_ref, gate_ref, up_ref, emit):
+    chips = arrived_ref.shape[0] // 8
+    part = arrived_ref.shape[1]
     pieces = 8 // CAP
-    to = iota((8 * chips, 8 * chips), 0)
-    at = 8 * (to % chips) + pieces * (to // chips % CAP) + to // (CAP * chips)
-    perm = (iota((8 * chips, 8 * chips), 1) == at).astype(F32).astype(BF16)
-    moved = jnp.dot(perm, moved, preferred_element_type=F32).astype(BF16)
-    for j in range(pieces):
-        rows_ref[:, j * part : (j + 1) * part] = moved[
-            j * CAP * chips : (j + 1) * CAP * chips
-        ]
+    some = min(chips, 32)
+    to = iota((8 * some, 1), 0)
+    at = 8 * (to % some) + pieces * (to // some % CAP) + to // (CAP * some)
+    perm = (iota((8 * some, 8 * some), 1) == at).astype(F32).astype(BF16)
+    for g in range(chips // some):
+        block = jnp.dot(
+            perm, arrived_ref[8 * some * g : 8 * some * (g + 1), :], preferred_element_type=F32
+        ).astype(BF16)
+        for s in range(CAP):
+            to_row = chips * s + some * g
+            for j in range(pieces):
+                from_row = some * (CAP * j + s)
+                rows_ref[to_row : to_row + some, j * part : (j + 1) * part] = block[
+                    from_row : from_row + some
+                ]
     units = gate_ref.shape[1] // pieces
     for q in range(units // TILE):
         for j in range(pieces):
@@ -91,12 +98,23 @@
             emit(q, k, hidden_ref[k].reshape(chips, 8, LANES).astype(BF16))
 
 
-def routed_own_kernel(own_ref, gate_ref, up_ref, out_ref, rows_ref, hidden_ref):
+def routed_own_kernel(
+    own_ref, gate_ref, up_ref, tokens_ref, partner_ref, out_ref, pair_ref, rows_ref, hidden_ref, sems
+):
+    copies = [
+        pltpu.make_async_copy(ref, pair_ref.at[i], sems.at[i])
+        for i, ref in enumerate((tokens_ref, partner_ref))
+    ]
+    for copy in copies:
+        copy.start()
+
     def emit(q, k, block):
         lane = q * TILE + k * LANES
         out_ref[:, :, lane : lane + LANES] = block
 
-    routed_rows(rows_ref, hidden_ref, own_ref[...], gate_ref, up_ref, emit)
+    routed_rows(rows_ref, hidden_ref, own_ref, gate_ref, up_ref, emit)
+    for copy in copies:
+        copy.wait()
 
 
 def routed_other_kernel(
@@ -120,45 +138,56 @@
             )
             copies[-1].start()
 
-    routed_rows(rows_ref, hidden_ref, other_ref[...], gate_ref, up_ref, emit)
+    routed_rows(rows_ref, hidden_ref, other_ref, gate_ref, up_ref, emit)
     first.wait()
     for copy in copies:
         copy.wait()
 
 
+def routed_work(chips, width):
+    return [
+        pltpu.VMEM((CAP * chips, width), BF16),
+        pltpu.VMEM((TILE // LANES, 8 * chips, LANES), F32),
+    ]
+
+
 def routed_estimate(rows, width, units):
     return pl.CostEstimate(flops=4 * rows * width * units, bytes_accessed=10**6, transcendentals=0)
 
 
-def routed(own, other, gate, up):
+def routed_own(own, gate, up, tokens, partner):
     rows, part = own.shape
     width, units = gate.shape
-    pieces = 8 // CAP
     chips = rows // 8
     vmem = pl.BlockSpec(memory_space=pltpu.VMEM)
     hbm = pl.BlockSpec(memory_space=pltpu.HBM)
-    work = [
-        pltpu.VMEM((CAP * chips, width), BF16),
-        pltpu.VMEM((TILE // LANES, 8 * chips, LANES), F32),
-    ]
-    block = (chips, 8, units // pieces)
-    mine = pl.pallas_call(
+    return pl.pallas_call(
         routed_own_kernel,
-        out_shape=pltpu.VMEM(block, BF16),
-        in_specs=[vmem] * 3,
-        out_specs=vmem,
-        scratch_shapes=work,
+        out_shape=(
+            pltpu.VMEM((chips, 8, units * CAP // 8), BF16),
+            jax.ShapeDtypeStruct((2,) + tokens.shape, BF16),
+        ),
+        in_specs=[vmem] * 3 + [hbm] * 2,
+        out_specs=(vmem, hbm),
+        scratch_shapes=routed_work(chips, width) + [pltpu.SemaphoreType.DMA((2,))],
         compiler_params=pltpu.CompilerParams(vmem_limit_bytes=12 << 20),
         name="routed_own",
         cost_estimate=routed_estimate(CAP * chips, width, units),
-    )(own, gate, up)
+    )(own, gate, up, tokens, partner)
+
+
+def routed_other(other, mine, gate, up):
+    width, units = gate.shape
+    chips = mine.shape[0]
+    vmem = pl.BlockSpec(memory_space=pltpu.VMEM)
+    hbm = pl.BlockSpec(memory_space=pltpu.HBM)
     return pl.pallas_call(
         routed_other_kernel,
-        out_shape=jax.ShapeDtypeStruct((chips, 2) + block[1:], BF16),
+        out_shape=jax.ShapeDtypeStruct((chips, 2) + mine.shape[1:], BF16),
         in_specs=[vmem] * 4,
         out_specs=hbm,
-        scratch_shapes=work
-        + [pltpu.VMEM(block, BF16), pltpu.SemaphoreType.DMA((units // pieces // TILE + 1,))],
+        scratch_shapes=routed_work(chips, width)
+        + [pltpu.VMEM(mine.shape, BF16), pltpu.SemaphoreType.DMA((mine.shape[2] // TILE + 1,))],
         compiler_params=pltpu.CompilerParams(vmem_limit_bytes=12 << 20),
         name="routed_other",
         cost_estimate=routed_estimate(CAP * chips, width, units),
@@ -170,38 +199,44 @@
     blocks = refs[:-3]
     core = lax.axis_index("core")
     y = lax.axis_index("y")
-    ring = len(blocks) // 2
+    step = 1 - 2 * core
     n = blocks[0].shape[0]
-    for c in range(2):
-        rows = jnp.concatenate([ref[...] for ref in blocks[ring * c : ring * (c + 1)]], axis=0)
+    ring = out_ref.shape[0] // (2 * n)
+    places = [
+        [(0, 0), (0, 1), (-1, 0), (-1, 1)],
+        [(1, 1), (1, 0), (2, 0), (2, 1)],
+    ]
+    for group, place in ((blocks[:3], places[0]), (blocks[3:], places[1])):
+        rows = jnp.concatenate(
+            [ref[...].reshape(-1, ref.shape[-1]) for ref in group], axis=0
+        )
         gate = jnp.dot(rows, gate_ref[...], preferred_element_type=F32)
         up = jnp.dot(rows, up_ref[...], preferred_element_type=F32)
         hidden = silu_mul(gate, up).astype(BF16)
-        core_of = core if c == 0 else 1 - core
-        step = 1 - 2 * core_of
-        for i, back in enumerate((0, 1, -1, 2)):
-            from_y = lax.rem(y - back * step + 2 * ring, ring)
-            at = pl.multiple_of(n * (2 * from_y + core_of), 16)
+        for i, (ahead, flip) in enumerate(place):
+            from_y = lax.rem(y + ahead * step + 2 * ring, ring)
+            from_core = 1 - core if flip else core
+            at = pl.multiple_of(n * (2 * from_y + from_core), 16)
             out_ref[pl.ds(at, n), :] = hidden[n * i : n * (i + 1)]
 
 
-def shared(blocks, shared_gate, shared_up):
-    n, width = blocks[0].shape
-    units = shared_gate.shape[1]
+def whole_block(x):
+    return pl.BlockSpec(x.shape, lambda q: (0,) * x.ndim)
+
+
+def shared(blocks, shared_gate, shared_up, rows):
+    width, units = shared_gate.shape
     tile = 256
-    whole = pl.BlockSpec((n, width), lambda q: (0, 0))
     weight = pl.BlockSpec((width, tile), lambda q: (0, q))
     return pl.pallas_call(
         shared_kernel,
-        out_shape=jax.ShapeDtypeStruct((len(blocks) * n, units), BF16),
+        out_shape=jax.ShapeDtypeStruct((rows, units), BF16),
         grid=(units // tile,),
-        in_specs=[whole] * len(blocks) + [weight, weight],
-        out_specs=pl.BlockSpec((len(blocks) * n, tile), lambda q: (0, q)),
+        in_specs=[whole_block(block) for block in blocks] + [weight, weight],
+        out_specs=pl.BlockSpec((rows, tile), lambda q: (0, q)),
         compiler_params=pltpu.CompilerParams(vmem_limit_bytes=32 << 20),
         name="shared",
-        cost_estimate=pl.CostEstimate(
-            flops=7 * 10**9, bytes_accessed=8 * 10**6, transcendentals=0
-        ),
+        cost_estimate=pl.CostEstimate(flops=5 * 10**9, bytes_accessed=8 * 10**6, transcendentals=0),
     )(*blocks, shared_gate, shared_up)
 
 
@@ -244,17 +279,17 @@
     return lax.ppermute(x, "core", [(0, 1), (1, 0)])
 
 
-def turn(x, ring, step):
-    pairs = [
-        (2 * y + c, 2 * ((y + step * (1 - 2 * c)) % ring) + c) for y in range(ring) for c in range(2)
-    ]
+def turn(x, ring):
+    pairs = [(2 * y + c, 2 * ((y + 1 - 2 * c) % ring) + c) for y in range(ring) for c in range(2)]
     return lax.ppermute(x, ("y", "core"), pairs)
 
 
 def shards(tokens, scores, expert_ids, gate_halves, up_halves, shared_gate, shared_up):
     ring = lax.axis_size("y")
     chips = lax.axis_size("wide") * ring
+    partner = swap(tokens)
     send = dispatch(tokens, scores, expert_ids, chips)
+    send, partner = lax.optimization_barrier((send, partner))
     arrived = lax.all_to_all(
         send.reshape(chips, 8, send.shape[1]), ("wide", "y"), split_axis=0, concat_axis=0, tiled=True
     ).reshape(send.shape)
@@ -262,10 +297,10 @@
     up = pltpu.with_memory_space_constraint(up_halves[0], pltpu.VMEM)
     arrived, mine = lax.optimization_barrier((arrived, tokens))
     arrived_other = swap(arrived)
-    after = turn(mine, ring, 1)
-    before = turn(mine, ring, -1)
-    opposite = turn(mine, ring, 2)
-    hidden = routed(arrived, arrived_other, gate, up)
+    opposite = lax.ppermute(mine, "y", [(y, (y + ring // 2) % ring) for y in range(ring)])
+    own_hidden, pair = routed_own(arrived, gate, up, mine, partner)
+    turned = turn(pair, ring)
+    hidden = routed_other(arrived_other, own_hidden, gate, up)
     back = lax.all_to_all(
         hidden.reshape(2 * chips, 8, hidden.shape[3]),
         ("wide", "y", "core"),
@@ -273,10 +308,9 @@
         concat_axis=0,
         tiled=True,
     ).reshape(16 * chips, hidden.shape[3])
-    blocks = [tokens, after, before, opposite]
-    blocks = blocks + [swap(block) for block in blocks]
-    blocks = lax.optimization_barrier((*blocks, hidden))[:-1]
-    shared_hidden = shared(blocks, shared_gate, shared_up)
+    turned, opposite, _ = lax.optimization_barrier((turned, opposite, hidden))
+    blocks = (tokens, partner, turned, swap(turned), opposite, swap(opposite))
+    shared_hidden = shared(blocks, shared_gate, shared_up, 2 * ring * tokens.shape[0])
     back, shared_hidden = lax.optimization_barrier((back, shared_hidden))
     return collect(back, expert_ids), shared_hidden
 

time: 67.5 us -> 66.2 us (0.981)
  waiting for transfers between devices: 9.41 us -> 2.88 us
  starting transfers between devices: 13 us -> 17.9 us
    ppermute x5 -> x4, starting transfers between devices: 4.13 us -> 11.7 us  [swap(): return lax.ppermute(x, 'core', [(0, 1), (1, 0)])]
    all_to_all x1, waiting for transfers between devices: 7.8 us -> 0.94 us  [shards(): lax.all_to_all(hidden.reshape(2 * chips, 8, hidden.shape[3]), ('wide', 'y...]
    all_to_all x1, starting transfers between devices: 6.67 us -> 4.03 us  [shards(): lax.all_to_all(hidden.reshape(2 * chips, 8, hidden.shape[3]), ('wide', 'y...]
    ppermute x0 -> x1, starting transfers between devices: none -> 1.87 us  [shards(): lax.ppermute(mine, 'y', [(y, (y + ring // 2) % ring) for y in range(ring)])]
    ppermute x3 -> x1, starting transfers between devices: 2.19 us -> 0.38 us  [turn(): return lax.ppermute(x, ('y', 'core'), pairs)]
    ppermute x5 -> x4, waiting for transfers between devices: 1.6 us -> 1.85 us  [swap(): return lax.ppermute(x, 'core', [(0, 1), (1, 0)])]
    unnamed x10 -> x12, local copies, waits for them, and re-layouts: 3.49 us -> 3.5 us
  transfers between devices with their start and end apart: 9 -> 7, of which waited for: 5 -> 3; matrix products, arithmetic and copies ran while one was open for 0% -> 0% of each run, Pallas kernels for 18% -> 21%
where the time goes in v3:
time: 66.2 us; the launch traced here: 65.9 us
  blocking collectives  25.5 us (39%)
  starting transfers between devices  17.9 us (27%)
  Pallas kernels  15.4 us (23%)
  local copies, waits for them, and re-layouts  3.5 us (5%)
  waiting for transfers between devices  2.88 us (4%)
  between operations  0.72 us (1%)
    all_to_all x1, blocking collectives, shards(): lax.all_to_all(send.reshape(chips, 8, send.shape[1]), ('wide', 'y'), spli...  25.5 us
    ppermute x4, starting transfers between devices, swap(): return lax.ppermute(x, 'core', [(0, 1), (1, 0)])  11.7 us
    pallas_call x1, Pallas kernels, routed_other(): pl.pallas_call(routed_other_kernel, out_shape=jax.ShapeDtypeStruct((chips...  4.26 us
    pallas_call x1, Pallas kernels, routed_own(): pl.pallas_call(routed_own_kernel, out_shape=(pltpu.VMEM((chips, 8, units...  4.03 us
    all_to_all x1, starting transfers between devices, shards(): lax.all_to_all(hidden.reshape(2 * chips, 8, hidden.shape[3]), ('wide', 'y...  4.03 us
    unnamed x12, local copies, waits for them, and re-layouts  3.5 us
    pallas_call x1, Pallas kernels, shared(): pl.pallas_call(shared_kernel, out_shape=jax.ShapeDtypeStruct((rows, units...  3.47 us
    pallas_call x1, Pallas kernels, dispatch(): pl.pallas_call(dispatch_kernel, out_shape=jax.ShapeDtypeStruct((chips * 8...  2.19 us
  transfers between devices with their start and end apart: 7, of which 3 were waited for; matrix products, arithmetic and copies ran while one was open for 0% of the time, Pallas kernels for 21%

profile of v3, /device:TPU:1, one launch (start us, length us, event | category | flops | bytes accessed | tf_op | source)
XLA Modules:
  0.0 65.9 jit_solution(14699099035235000357)
XLA Ops:
  0.7 1.5 %collective-permute-start = (bf16[48,2560]{1,0:T(8,128)(2,1)}, bf16[48,2560]{1,0:T(8,128)(2,1)S(1)}, u32[]{:S(2)}, u32[]{:S(2)}) collective-permute-start(bf16[48,2560]{1,0:T(8,128)(2,1)} %refs_0_.1), channel_id=1, source_target_pairs={{0,1},{1,0},{2,3},{3,2},{4,5},{5,4},{6,7},{7,6},{8,9},{9,8},{10,11... | collective-permute-start | bytes 737288 | tf_op jit(solution)/shard_map/ppermute | solution.py:279
  2.2 2.2 %dispatch.1 = bf16[512,640]{1,0:T(8,128)(2,1)S(1)} custom-call(bf16[48,2560]{1,0:T(8,128)(2,1)} %refs_0_.1, f32[48]{0:T(128)} %scores_ref.1, s32[48]{0:T(128)} %ids_ref.3), custom_call_target="tpu_custom_call" | custom-call | flops 20000000000 | bytes 2000000 | tf_op jit(solution)/shard_map/dispatch/pallas_call | solution.py:47
  4.4 0.0 collective-permute-done.partner_ref.refs_1_
  4.4 25.5 %all_to_all.10 = bf16[64,8,640]{2,1,0:T(8,128)(2,1)S(1)} all-to-all(bf16[64,8,640]{2,1,0:T(8,128)(2,1)S(1)} %bitcast.13), channel_id=1, replica_groups=mesh['wide'=16,'y'=4,'core'=2] {'wide','y'}, dimensions={0} | all-to-all | bytes 1310720 | tf_op jit(solution)/shard_map/all_to_all | solution.py:293
  29.9 1.1 %collective-permute-start.1 = (bf16[512,640]{1,0:T(8,128)(2,1)S(1)}, bf16[512,640]{1,0:T(8,128)(2,1)S(1)}, u32[]{:S(2)}, u32[]{:S(2)}) collective-permute-start(bf16[512,640]{1,0:T(8,128)(2,1)S(1)} %bitcast.10), channel_id=1, source_target_pairs={{0,1},{1,0},{2,3},{3,2},{4,5},{5,4},{6,7},{7,6},{8,9},{9,8},{10,11... | collective-permute-start | bytes 1966088 | tf_op jit(solution)/shard_map/ppermute | solution.py:279
  30.9 0.0 copy-done
  31.0 4.0 %routed_own.1 = (bf16[64,8,512]{2,1,0:T(8,128)(2,1)S(1)}, bf16[2,48,2560]{2,1,0:T(8,128)(2,1)S(1)}) custom-call(bf16[512,640]{1,0:T(8,128)(2,1)S(1)} %bitcast.11, bf16[2560,2048]{1,0:T(8,128)(2,1)S(1)} %bitcast.6, bf16[2560,2048]{1,0:T(8,128)(2,1)S(1)} %bitcast.8, bf16[48,2560]{1,0:T(8,128)(2,1)S(1)} %copy-done.2, ...), custom_call_target="tpu_custom_call" | custom-call | flops 2684354560 | bytes 1000000 | tf_op jit(solution)/shard_map/routed_own/pallas_call | solution.py:164
  35.0 0.4 collective-permute-start.2
  35.4 1.9 %collective-permute-start.3 = (bf16[48,2560]{1,0:T(8,128)(2,1)S(1)}, bf16[48,2560]{1,0:T(8,128)(2,1)S(1)}, u32[]{:S(2)}, u32[]{:S(2)}) collective-permute-start(bf16[48,2560]{1,0:T(8,128)(2,1)S(1)} %copy-done.2), channel_id=1, source_target_pairs={{0,4},{2,6},{4,0},{6,2},{1,5},{3,7},{5,1},{7,3},{8,12},{10,14},{12... | collective-permute-start | bytes 737288 | tf_op jit(solution)/shard_map/ppermute | solution.py:300
  37.3 0.0 collective-permute-done.1.other_ref
  37.3 4.3 %routed_other.1 = bf16[64,2,8,512]{3,2,1,0:T(8,128)(2,1)} custom-call(bf16[512,640]{1,0:T(8,128)(2,1)S(1)} %collective-permute-done.1.other_ref, bf16[64,8,512]{2,1,0:T(8,128)(2,1)S(1)} %get-tuple-element.16.mine_ref, bf16[2560,2048]{1,0:T(8,128)(2,1)S(1)} %bitcast.7, bf16[2560,2048]{1,0:T(8,128)(2,1)S(1)} %bitcast.9), custom_call_target="tpu_custom_call" | custom-call | flops 2684354560 | bytes 1000000 | tf_op jit(solution)/shard_map/routed_other/pallas_call | solution.py:184
  41.5 0.0 copy-start.5
  41.5 4.0 %all-to-all-start.1 = ((bf16[128,8,512]{2,1,0:T(8,128)(2,1)}), bf16[128,8,512]{2,1,0:T(8,128)(2,1)S(1)}, u32[]{:S(2)}, u32[]{:S(2)}) async-start(bf16[128,8,512]{2,1,0:T(8,128)(2,1)} %bitcast.4), calls=%async_computation.1 | async-start | bytes 2097152 | tf_op jit(solution)/shard_map/all_to_all | solution.py:304
  45.6 0.0 collective-permute-done.3.refs_4_
  45.6 0.1 collective-permute-done.2.refs_2_
  45.7 9.1 %collective-permute-start.4 = (bf16[2,48,2560]{2,1,0:T(8,128)(2,1)S(1)}, bf16[2,48,2560]{2,1,0:T(8,128)(2,1)S(1)}, u32[]{:S(2)}, u32[]{:S(2)}) collective-permute-start(bf16[2,48,2560]{2,1,0:T(8,128)(2,1)S(1)} %collective-permute-done.2.refs_2_), channel_id=1, source_target_pairs={{0,1},{1,0},{2,3},{3,2},{4,5},{5,4},{6,7},{7,6},{8,9},{9,8},{10,11... | collective-permute-start | bytes 1474568 | tf_op jit(solution)/shard_map/ppermute | solution.py:279
  54.7 0.0 collective-permute-start.5
  54.7 1.8 %collective-permute-done.5.refs_5_ = bf16[48,2560]{1,0:T(8,128)(2,1)S(1)} collective-permute-done((bf16[48,2560]{1,0:T(8,128)(2,1)S(1)}, bf16[48,2560]{1,0:T(8,128)(2,1)S(1)}, u32[]{:S(2)}, u32[]{:S(2)}) %collective-permute-start.5) | collective-permute-done | bytes 245792 | tf_op jit(solution)/shard_map/ppermute | solution.py:279
  56.6 0.0 collective-permute-done.4.refs_3_
  56.6 1.7 %copy-done.3 = bf16[2560,512]{1,0:T(8,128)(2,1)S(1)} copy-done((bf16[2560,512]{1,0:T(8,128)(2,1)S(1)}, bf16[2560,512]{1,0:T(8,128)(2,1)}, u32[]{:S(2)}) %copy-start.3) | copy-done | bytes 2621464
  58.3 1.7 %copy-done.4 = bf16[2560,512]{1,0:T(8,128)(2,1)S(1)} copy-done((bf16[2560,512]{1,0:T(8,128)(2,1)S(1)}, bf16[2560,512]{1,0:T(8,128)(2,1)}, u32[]{:S(2)}) %copy-start.4) | copy-done | bytes 2621464
  60.1 3.5 %shared.1 = bf16[384,512]{1,0:T(8,128)(2,1)} custom-call(bf16[48,2560]{1,0:T(8,128)(2,1)S(1)} %copy-done.2, bf16[48,2560]{1,0:T(8,128)(2,1)S(1)} %collective-permute-done.partner_ref.refs_1_, bf16[2,48,2560]{2,1,0:T(8,128)(2,1)S(1)} %collective-permute-done.2.refs_2_, bf16[2,48,2560]{2,1,0:T(8,128)(2,1)S(1)} %collective-permute-done.4.refs_3_, ...), custom_call_target="tpu_custom_call" | custom-call | flops 5000000000 | bytes 8000000 | tf_op jit(solution)/shard_map/shared/pallas_call | solution.py:231
  63.5 0.9 %all-to-all-done.1 = bf16[128,8,512]{2,1,0:T(8,128)(2,1)S(1)} async-done(((bf16[128,8,512]{2,1,0:T(8,128)(2,1)}), bf16[128,8,512]{2,1,0:T(8,128)(2,1)S(1)}, u32[]{:S(2)}, u32[]{:S(2)}) %all-to-all-start.1) | async-done | bytes 1048608 | tf_op jit(solution)/shard_map/all_to_all | solution.py:304
  64.5 1.5 %collect.1 = bf16[48,4096]{1,0:T(8,128)(2,1)} custom-call(bf16[1024,512]{1,0:T(8,128)(2,1)S(1)} %bitcast.12, s32[48]{0:T(128)S(1)} %copy-done.5), custom_call_target="tpu_custom_call" | custom-call | flops 400000000 | bytes 1500000 | tf_op jit(solution)/shard_map/collect/pallas_call | solution.py:269
  (8 shorter events, 0.0 us)
Async XLA Ops:
  0.6 30.3 %copy-start.2 = (bf16[48,2560]{1,0:T(8,128)(2,1)S(1)}, bf16[48,2560]{1,0:T(8,128)(2,1)}, u32[]{:S(2)}) copy-start(bf16[48,2560]{1,0:T(8,128)(2,1)} %refs_0_.1) | copy-start | bytes 737284
  0.6 30.3 %copy-start = (bf16[1,2560,2048]{2,1,0:T(8,128)(2,1)S(1)}, bf16[1,2560,2048]{2,1,0:T(8,128)(2,1)}, u32[]{:S(2)}) copy-start(bf16[1,2560,2048]{2,1,0:T(8,128)(2,1)} %param.10) | copy-start | bytes 31457284
  0.7 30.3 %copy-start.1 = (bf16[1,2560,2048]{2,1,0:T(8,128)(2,1)S(1)}, bf16[1,2560,2048]{2,1,0:T(8,128)(2,1)}, u32[]{:S(2)}) copy-start(bf16[1,2560,2048]{2,1,0:T(8,128)(2,1)} %param.11) | copy-start | bytes 31457284
  0.7 3.7 %collective-permute-start = (bf16[48,2560]{1,0:T(8,128)(2,1)}, bf16[48,2560]{1,0:T(8,128)(2,1)S(1)}, u32[]{:S(2)}, u32[]{:S(2)}) collective-permute-start(bf16[48,2560]{1,0:T(8,128)(2,1)} %refs_0_.1), channel_id=1, source_target_pairs={{0,1},{1,0},{2,3},{3,2},{4,5},{5,4},{6,7},{7,6},{8,9},{9,8},{10,11... | collective-permute-start | bytes 737288 | tf_op jit(solution)/shard_map/ppermute | solution.py:279
  29.9 7.4 %collective-permute-start.1 = (bf16[512,640]{1,0:T(8,128)(2,1)S(1)}, bf16[512,640]{1,0:T(8,128)(2,1)S(1)}, u32[]{:S(2)}, u32[]{:S(2)}) collective-permute-start(bf16[512,640]{1,0:T(8,128)(2,1)S(1)} %bitcast.10), channel_id=1, source_target_pairs={{0,1},{1,0},{2,3},{3,2},{4,5},{5,4},{6,7},{7,6},{8,9},{9,8},{10,11... | collective-permute-start | bytes 1966088 | tf_op jit(solution)/shard_map/ppermute | solution.py:279
  35.0 10.7 %collective-permute-start.2 = (bf16[2,48,2560]{2,1,0:T(8,128)(2,1)S(1)}, bf16[2,48,2560]{2,1,0:T(8,128)(2,1)S(1)}, u32[]{:S(2)}, u32[]{:S(2)}) collective-permute-start(bf16[2,48,2560]{2,1,0:T(8,128)(2,1)S(1)} %get-tuple-element.17), channel_id=1, source_target_pairs={{0,2},{1,7},{2,4},{3,1},{4,6},{5,3},{6,0},{7,5},{8,10},{9,15},{10,... | collective-permute-start | bytes 1474568 | tf_op jit(solution)/shard_map/ppermute | solution.py:284
  35.4 10.2 %collective-permute-start.3 = (bf16[48,2560]{1,0:T(8,128)(2,1)S(1)}, bf16[48,2560]{1,0:T(8,128)(2,1)S(1)}, u32[]{:S(2)}, u32[]{:S(2)}) collective-permute-start(bf16[48,2560]{1,0:T(8,128)(2,1)S(1)} %copy-done.2), channel_id=1, source_target_pairs={{0,4},{2,6},{4,0},{6,2},{1,5},{3,7},{5,1},{7,3},{8,12},{10,14},{12... | collective-permute-start | bytes 737288 | tf_op jit(solution)/shard_map/ppermute | solution.py:300
  41.5 23.0 %copy-start.5 = (s32[48]{0:T(128)S(1)}, s32[48]{0:T(128)}, u32[]{:S(2)}) copy-start(s32[48]{0:T(128)} %ids_ref.3) | copy-start | bytes 580
  41.5 22.9 %all-to-all-start.1 = ((bf16[128,8,512]{2,1,0:T(8,128)(2,1)}), bf16[128,8,512]{2,1,0:T(8,128)(2,1)S(1)}, u32[]{:S(2)}, u32[]{:S(2)}) async-start(bf16[128,8,512]{2,1,0:T(8,128)(2,1)} %bitcast.4), calls=%async_computation.1 | async-start | bytes 2097152 | tf_op jit(solution)/shard_map/all_to_all | solution.py:304
  45.7 10.9 %collective-permute-start.4 = (bf16[2,48,2560]{2,1,0:T(8,128)(2,1)S(1)}, bf16[2,48,2560]{2,1,0:T(8,128)(2,1)S(1)}, u32[]{:S(2)}, u32[]{:S(2)}) collective-permute-start(bf16[2,48,2560]{2,1,0:T(8,128)(2,1)S(1)} %collective-permute-done.2.refs_2_), channel_id=1, source_target_pairs={{0,1},{1,0},{2,3},{3,2},{4,5},{5,4},{6,7},{7,6},{8,9},{9,8},{10,11... | collective-permute-start | bytes 1474568 | tf_op jit(solution)/shard_map/ppermute | solution.py:279
  54.7 1.8 %collective-permute-start.5 = (bf16[48,2560]{1,0:T(8,128)(2,1)S(1)}, bf16[48,2560]{1,0:T(8,128)(2,1)S(1)}, u32[]{:S(2)}, u32[]{:S(2)}) collective-permute-start(bf16[48,2560]{1,0:T(8,128)(2,1)S(1)} %collective-permute-done.3.refs_4_), channel_id=1, source_target_pairs={{0,1},{1,0},{2,3},{3,2},{4,5},{5,4},{6,7},{7,6},{8,9},{9,8},{10,11... | collective-permute-start | bytes 737288 | tf_op jit(solution)/shard_map/ppermute | solution.py:279
  56.6 1.7 %copy-start.3 = (bf16[2560,512]{1,0:T(8,128)(2,1)S(1)}, bf16[2560,512]{1,0:T(8,128)(2,1)}, u32[]{:S(2)}) copy-start(bf16[2560,512]{1,0:T(8,128)(2,1)} %refs_6_.1) | copy-start | bytes 7864324
  58.3 1.7 %copy-start.4 = (bf16[2560,512]{1,0:T(8,128)(2,1)S(1)}, bf16[2560,512]{1,0:T(8,128)(2,1)}, u32[]{:S(2)}) copy-start(bf16[2560,512]{1,0:T(8,128)(2,1)} %refs_7_.1) | copy-start | bytes 7864324

commit v4 on v3

--- a/solution.py
+++ b/solution.py
@@ -34,10 +34,8 @@
     earlier = (ids_col == ids_row) & (iota((n, n), 0) < iota((n, n), 1))
     rank_row = jnp.sum(earlier.astype(I32), axis=0, keepdims=True)
     entry = 8 * ids_row + pieces * rank_row
-    rows = iota((send_ref.shape[0], n), 0)
-    hot = jnp.concatenate(
-        [(rows == entry + j).astype(F32).astype(BF16) for j in range(pieces)], axis=1
-    )
+    entries = jnp.concatenate([entry + j for j in range(pieces)], axis=1)
+    hot = (iota((send_ref.shape[0], pieces * n), 0) == entries).astype(F32).astype(BF16)
     stack = jnp.concatenate([scaled[:, j * part : (j + 1) * part] for j in range(pieces)], axis=0)
     send_ref[...] = jnp.dot(hot, stack, preferred_element_type=F32).astype(BF16)
 
@@ -165,7 +163,7 @@
         routed_own_kernel,
         out_shape=(
             pltpu.VMEM((chips, 8, units * CAP // 8), BF16),
-            jax.ShapeDtypeStruct((2,) + tokens.shape, BF16),
+            pltpu.HBM((2,) + tokens.shape, BF16),
         ),
         in_specs=[vmem] * 3 + [hbm] * 2,
         out_specs=(vmem, hbm),
@@ -237,7 +235,11 @@
         compiler_params=pltpu.CompilerParams(vmem_limit_bytes=32 << 20),
         name="shared",
         cost_estimate=pl.CostEstimate(flops=5 * 10**9, bytes_accessed=8 * 10**6, transcendentals=0),
-    )(*blocks, shared_gate, shared_up)
+    )(
+        *blocks,
+        pltpu.with_memory_space_constraint(shared_gate, pltpu.HBM),
+        pltpu.with_memory_space_constraint(shared_up, pltpu.HBM),
+    )
 
 
 def collect_kernel(back_ref, ids_ref, out_ref):

time: 66.2 us -> 65.5 us (0.989)
  local copies, waits for them, and re-layouts: 3.5 us -> 0.02 us
  starting transfers between devices: 17.9 us -> 20.5 us
  Pallas kernels: 15.4 us -> 16.1 us
    unnamed x12 -> x8, local copies, waits for them, and re-layouts: 3.5 us -> 0.02 us
    ppermute x4, starting transfers between devices: 11.7 us -> 14.2 us  [swap(): return lax.ppermute(x, 'core', [(0, 1), (1, 0)])]
    pallas_call x1, Pallas kernels: 3.47 us -> 4.83 us  [shared(): pl.pallas_call(shared_kernel, out_shape=jax.ShapeDtypeStruct((rows, units...]
  transfers between devices with their start and end apart: 7 -> 7, of which waited for: 3 -> 3; matrix products, arithmetic and copies ran while one was open for 0% -> 0% of each run, Pallas kernels for 21% -> 22%
where the time goes in v4:
time: 65.5 us; the launch traced here: 65.3 us
  blocking collectives  25.1 us (38%)
  starting transfers between devices  20.5 us (31%)
  Pallas kernels  16.1 us (25%)
  waiting for transfers between devices  2.79 us (4%)
  between operations  0.72 us (1%)
    all_to_all x1, blocking collectives, shards(): lax.all_to_all(send.reshape(chips, 8, send.shape[1]), ('wide', 'y'), spli...  25.1 us
    ppermute x4, starting transfers between devices, swap(): return lax.ppermute(x, 'core', [(0, 1), (1, 0)])  14.2 us
    pallas_call x1, Pallas kernels, shared(): pl.pallas_call(shared_kernel, out_shape=jax.ShapeDtypeStruct((rows, units...  4.83 us
    pallas_call x1, Pallas kernels, routed_other(): pl.pallas_call(routed_other_kernel, out_shape=jax.ShapeDtypeStruct((chips...  4.25 us
    all_to_all x1, starting transfers between devices, shards(): lax.all_to_all(hidden.reshape(2 * chips, 8, hidden.shape[3]), ('wide', 'y...  4.03 us
    pallas_call x1, Pallas kernels, routed_own(): pl.pallas_call(routed_own_kernel, out_shape=(pltpu.VMEM((chips, 8, units...  3.43 us
    pallas_call x1, Pallas kernels, dispatch(): pl.pallas_call(dispatch_kernel, out_shape=jax.ShapeDtypeStruct((chips * 8...  2.16 us
    ppermute x1, starting transfers between devices, shards(): lax.ppermute(mine, 'y', [(y, (y + ring // 2) % ring) for y in range(ring)])  1.96 us
  transfers between devices with their start and end apart: 7, of which 3 were waited for; matrix products, arithmetic and copies ran while one was open for 0% of the time, Pallas kernels for 22%

profile of v4, /device:TPU:1, one launch (start us, length us, event | category | flops | bytes accessed | tf_op | source)
XLA Modules:
  0.0 65.3 jit_solution(11038338614944347886)
XLA Ops:
  0.6 0.0 copy-start.2
  0.6 0.0 copy-start
  0.7 0.0 copy-start.1
  0.7 1.5 %collective-permute-start = (bf16[48,2560]{1,0:T(8,128)(2,1)}, bf16[48,2560]{1,0:T(8,128)(2,1)S(1)}, u32[]{:S(2)}, u32[]{:S(2)}) collective-permute-start(bf16[48,2560]{1,0:T(8,128)(2,1)} %refs_0_.1), channel_id=1, source_target_pairs={{0,1},{1,0},{2,3},{3,2},{4,5},{5,4},{6,7},{7,6},{8,9},{9,8},{10,11... | collective-permute-start | bytes 737288 | tf_op jit(solution)/shard_map/ppermute | solution.py:281
  2.2 2.2 %dispatch.1 = bf16[512,640]{1,0:T(8,128)(2,1)S(1)} custom-call(bf16[48,2560]{1,0:T(8,128)(2,1)} %refs_0_.1, f32[48]{0:T(128)} %scores_ref.1, s32[48]{0:T(128)} %ids_ref.3), custom_call_target="tpu_custom_call" | custom-call | flops 20000000000 | bytes 2000000 | tf_op jit(solution)/shard_map/dispatch/pallas_call | solution.py:45
  4.3 0.0 collective-permute-done.partner_ref.refs_1_
  4.3 25.1 %all_to_all.10 = bf16[64,8,640]{2,1,0:T(8,128)(2,1)S(1)} all-to-all(bf16[64,8,640]{2,1,0:T(8,128)(2,1)S(1)} %bitcast.13), channel_id=1, replica_groups=mesh['wide'=16,'y'=4,'core'=2] {'wide','y'}, dimensions={0} | all-to-all | bytes 1310720 | tf_op jit(solution)/shard_map/all_to_all | solution.py:295
  29.4 1.5 %collective-permute-start.1 = (bf16[512,640]{1,0:T(8,128)(2,1)S(1)}, bf16[512,640]{1,0:T(8,128)(2,1)S(1)}, u32[]{:S(2)}, u32[]{:S(2)}) collective-permute-start(bf16[512,640]{1,0:T(8,128)(2,1)S(1)} %bitcast.10), channel_id=1, source_target_pairs={{0,1},{1,0},{2,3},{3,2},{4,5},{5,4},{6,7},{7,6},{8,9},{9,8},{10,11... | collective-permute-start | bytes 1966088 | tf_op jit(solution)/shard_map/ppermute | solution.py:281
  30.9 3.4 %routed_own.1 = (bf16[64,8,512]{2,1,0:T(8,128)(2,1)S(1)}, bf16[2,48,2560]{2,1,0:T(8,128)(2,1)}) custom-call(bf16[512,640]{1,0:T(8,128)(2,1)S(1)} %bitcast.11, bf16[2560,2048]{1,0:T(8,128)(2,1)S(1)} %bitcast.6, bf16[2560,2048]{1,0:T(8,128)(2,1)S(1)} %bitcast.8, bf16[48,2560]{1,0:T(8,128)(2,1)S(1)} %copy-done.2, ...), custom_call_target="tpu_custom_call" | custom-call | flops 2684354560 | bytes 1000000 | tf_op jit(solution)/shard_map/routed_own/pallas_call | solution.py:162
  34.4 0.3 collective-permute-start.2
  34.7 2.0 %collective-permute-start.3 = (bf16[48,2560]{1,0:T(8,128)(2,1)S(1)}, bf16[48,2560]{1,0:T(8,128)(2,1)S(1)}, u32[]{:S(2)}, u32[]{:S(2)}) collective-permute-start(bf16[48,2560]{1,0:T(8,128)(2,1)S(1)} %copy-done.2), channel_id=1, source_target_pairs={{0,4},{2,6},{4,0},{6,2},{1,5},{3,7},{5,1},{7,3},{8,12},{10,14},{12... | collective-permute-start | bytes 737288 | tf_op jit(solution)/shard_map/ppermute | solution.py:302
  36.6 0.0 collective-permute-done.1.other_ref
  36.6 4.3 %routed_other.1 = bf16[64,2,8,512]{3,2,1,0:T(8,128)(2,1)} custom-call(bf16[512,640]{1,0:T(8,128)(2,1)S(1)} %collective-permute-done.1.other_ref, bf16[64,8,512]{2,1,0:T(8,128)(2,1)S(1)} %get-tuple-element.16.mine_ref, bf16[2560,2048]{1,0:T(8,128)(2,1)S(1)} %bitcast.7, bf16[2560,2048]{1,0:T(8,128)(2,1)S(1)} %bitcast.9), custom_call_target="tpu_custom_call" | custom-call | flops 2684354560 | bytes 1000000 | tf_op jit(solution)/shard_map/routed_other/pallas_call | solution.py:182
  40.9 0.0 copy-start.3
  40.9 4.0 %all-to-all-start.1 = ((bf16[128,8,512]{2,1,0:T(8,128)(2,1)}), bf16[128,8,512]{2,1,0:T(8,128)(2,1)S(1)}, u32[]{:S(2)}, u32[]{:S(2)}) async-start(bf16[128,8,512]{2,1,0:T(8,128)(2,1)} %bitcast.4), calls=%async_computation.1 | async-start | bytes 2097152 | tf_op jit(solution)/shard_map/all_to_all | solution.py:306
  44.9 0.0 collective-permute-done.3.refs_4_
  44.9 0.3 collective-permute-done.2.refs_2_
  45.2 11.3 %collective-permute-start.4 = (bf16[2,48,2560]{2,1,0:T(8,128)(2,1)S(1)}, bf16[2,48,2560]{2,1,0:T(8,128)(2,1)S(1)}, u32[]{:S(2)}, u32[]{:S(2)}) collective-permute-start(bf16[2,48,2560]{2,1,0:T(8,128)(2,1)S(1)} %collective-permute-done.2.refs_2_), channel_id=1, source_target_pairs={{0,1},{1,0},{2,3},{3,2},{4,5},{5,4},{6,7},{7,6},{8,9},{9,8},{10,11... | collective-permute-start | bytes 1474568 | tf_op jit(solution)/shard_map/ppermute | solution.py:281
  56.5 0.0 collective-permute-start.5
  56.5 1.8 %collective-permute-done.5.refs_5_ = bf16[48,2560]{1,0:T(8,128)(2,1)S(1)} collective-permute-done((bf16[48,2560]{1,0:T(8,128)(2,1)S(1)}, bf16[48,2560]{1,0:T(8,128)(2,1)S(1)}, u32[]{:S(2)}, u32[]{:S(2)}) %collective-permute-start.5) | collective-permute-done | bytes 245792 | tf_op jit(solution)/shard_map/ppermute | solution.py:281
  58.4 0.0 collective-permute-done.4.refs_3_
  58.4 4.8 %shared.1 = bf16[384,512]{1,0:T(8,128)(2,1)} custom-call(bf16[48,2560]{1,0:T(8,128)(2,1)S(1)} %copy-done.2, bf16[48,2560]{1,0:T(8,128)(2,1)S(1)} %collective-permute-done.partner_ref.refs_1_, bf16[2,48,2560]{2,1,0:T(8,128)(2,1)S(1)} %collective-permute-done.2.refs_2_, bf16[2,48,2560]{2,1,0:T(8,128)(2,1)S(1)} %collective-permute-done.4.refs_3_, ...), custom_call_target="tpu_custom_call" | custom-call | flops 5000000000 | bytes 8000000 | tf_op jit(solution)/shard_map/shared/pallas_call | solution.py:229
  63.2 0.6 all-to-all-done.1
  63.8 1.5 %collect.1 = bf16[48,4096]{1,0:T(8,128)(2,1)} custom-call(bf16[1024,512]{1,0:T(8,128)(2,1)S(1)} %bitcast.12, s32[48]{0:T(128)S(1)} %copy-done.3), custom_call_target="tpu_custom_call" | custom-call | flops 400000000 | bytes 1500000 | tf_op jit(solution)/shard_map/collect/pallas_call | solution.py:271
  (4 shorter events, 0.0 us)
Async XLA Ops:
  0.6 30.3 %copy-start.2 = (bf16[48,2560]{1,0:T(8,128)(2,1)S(1)}, bf16[48,2560]{1,0:T(8,128)(2,1)}, u32[]{:S(2)}) copy-start(bf16[48,2560]{1,0:T(8,128)(2,1)} %refs_0_.1) | copy-start | bytes 737284
  0.6 30.3 %copy-start = (bf16[1,2560,2048]{2,1,0:T(8,128)(2,1)S(1)}, bf16[1,2560,2048]{2,1,0:T(8,128)(2,1)}, u32[]{:S(2)}) copy-start(bf16[1,2560,2048]{2,1,0:T(8,128)(2,1)} %param.10) | copy-start | bytes 31457284
  0.7 30.3 %copy-start.1 = (bf16[1,2560,2048]{2,1,0:T(8,128)(2,1)S(1)}, bf16[1,2560,2048]{2,1,0:T(8,128)(2,1)}, u32[]{:S(2)}) copy-start(bf16[1,2560,2048]{2,1,0:T(8,128)(2,1)} %param.11) | copy-start | bytes 31457284
  0.7 3.7 %collective-permute-start = (bf16[48,2560]{1,0:T(8,128)(2,1)}, bf16[48,2560]{1,0:T(8,128)(2,1)S(1)}, u32[]{:S(2)}, u32[]{:S(2)}) collective-permute-start(bf16[48,2560]{1,0:T(8,128)(2,1)} %refs_0_.1), channel_id=1, source_target_pairs={{0,1},{1,0},{2,3},{3,2},{4,5},{5,4},{6,7},{7,6},{8,9},{9,8},{10,11... | collective-permute-start | bytes 737288 | tf_op jit(solution)/shard_map/ppermute | solution.py:281
  29.4 7.2 %collective-permute-start.1 = (bf16[512,640]{1,0:T(8,128)(2,1)S(1)}, bf16[512,640]{1,0:T(8,128)(2,1)S(1)}, u32[]{:S(2)}, u32[]{:S(2)}) collective-permute-start(bf16[512,640]{1,0:T(8,128)(2,1)S(1)} %bitcast.10), channel_id=1, source_target_pairs={{0,1},{1,0},{2,3},{3,2},{4,5},{5,4},{6,7},{7,6},{8,9},{9,8},{10,11... | collective-permute-start | bytes 1966088 | tf_op jit(solution)/shard_map/ppermute | solution.py:281
  34.4 10.9 %collective-permute-start.2 = (bf16[2,48,2560]{2,1,0:T(8,128)(2,1)}, bf16[2,48,2560]{2,1,0:T(8,128)(2,1)S(1)}, u32[]{:S(2)}, u32[]{:S(2)}) collective-permute-start(bf16[2,48,2560]{2,1,0:T(8,128)(2,1)} %get-tuple-element.17), channel_id=1, source_target_pairs={{0,2},{1,7},{2,4},{3,1},{4,6},{5,3},{6,0},{7,5},{8,10},{9,15},{10,... | collective-permute-start | bytes 1474568 | tf_op jit(solution)/shard_map/ppermute | solution.py:286
  34.7 10.3 %collective-permute-start.3 = (bf16[48,2560]{1,0:T(8,128)(2,1)S(1)}, bf16[48,2560]{1,0:T(8,128)(2,1)S(1)}, u32[]{:S(2)}, u32[]{:S(2)}) collective-permute-start(bf16[48,2560]{1,0:T(8,128)(2,1)S(1)} %copy-done.2), channel_id=1, source_target_pairs={{0,4},{2,6},{4,0},{6,2},{1,5},{3,7},{5,1},{7,3},{8,12},{10,14},{12... | collective-permute-start | bytes 737288 | tf_op jit(solution)/shard_map/ppermute | solution.py:302
  40.9 23.0 %copy-start.3 = (s32[48]{0:T(128)S(1)}, s32[48]{0:T(128)}, u32[]{:S(2)}) copy-start(s32[48]{0:T(128)} %ids_ref.3) | copy-start | bytes 580
  40.9 22.9 %all-to-all-start.1 = ((bf16[128,8,512]{2,1,0:T(8,128)(2,1)}), bf16[128,8,512]{2,1,0:T(8,128)(2,1)S(1)}, u32[]{:S(2)}, u32[]{:S(2)}) async-start(bf16[128,8,512]{2,1,0:T(8,128)(2,1)} %bitcast.4), calls=%async_computation.1 | async-start | bytes 2097152 | tf_op jit(solution)/shard_map/all_to_all | solution.py:306
  45.2 13.1 %collective-permute-start.4 = (bf16[2,48,2560]{2,1,0:T(8,128)(2,1)S(1)}, bf16[2,48,2560]{2,1,0:T(8,128)(2,1)S(1)}, u32[]{:S(2)}, u32[]{:S(2)}) collective-permute-start(bf16[2,48,2560]{2,1,0:T(8,128)(2,1)S(1)} %collective-permute-done.2.refs_2_), channel_id=1, source_target_pairs={{0,1},{1,0},{2,3},{3,2},{4,5},{5,4},{6,7},{7,6},{8,9},{9,8},{10,11... | collective-permute-start | bytes 1474568 | tf_op jit(solution)/shard_map/ppermute | solution.py:281
  56.5 1.8 %collective-permute-start.5 = (bf16[48,2560]{1,0:T(8,128)(2,1)S(1)}, bf16[48,2560]{1,0:T(8,128)(2,1)S(1)}, u32[]{:S(2)}, u32[]{:S(2)}) collective-permute-start(bf16[48,2560]{1,0:T(8,128)(2,1)S(1)} %collective-permute-done.3.refs_4_), channel_id=1, source_target_pairs={{0,1},{1,0},{2,3},{3,2},{4,5},{5,4},{6,7},{7,6},{8,9},{9,8},{10,11... | collective-permute-start | bytes 737288 | tf_op jit(solution)/shard_map/ppermute | solution.py:281

commit v5 on v4

--- a/solution.py
+++ b/solution.py
@@ -7,7 +7,7 @@
 
 CAP = 2
 LANES = 128
-TILE = 256
+TILE = 512
 F32 = jnp.float32
 BF16 = jnp.bfloat16
 I32 = jnp.int32

time: 65.5 us -> 65.5 us (level)
  no operation moved by 1% of the time
where the time goes in v5:
time: 65.5 us; the launch traced here: 65.3 us
  blocking collectives  25.1 us (38%)
  starting transfers between devices  20.5 us (31%)
  Pallas kernels  16.1 us (25%)
  waiting for transfers between devices  2.81 us (4%)
  between operations  0.72 us (1%)
    all_to_all x1, blocking collectives, shards(): lax.all_to_all(send.reshape(chips, 8, send.shape[1]), ('wide', 'y'), spli...  25.1 us
    ppermute x4, starting transfers between devices, swap(): return lax.ppermute(x, 'core', [(0, 1), (1, 0)])  14.2 us
    pallas_call x1, Pallas kernels, shared(): pl.pallas_call(shared_kernel, out_shape=jax.ShapeDtypeStruct((rows, units...  4.83 us
    pallas_call x1, Pallas kernels, routed_other(): pl.pallas_call(routed_other_kernel, out_shape=jax.ShapeDtypeStruct((chips...  4.27 us
    all_to_all x1, starting transfers between devices, shards(): lax.all_to_all(hidden.reshape(2 * chips, 8, hidden.shape[3]), ('wide', 'y...  4.03 us
    pallas_call x1, Pallas kernels, routed_own(): pl.pallas_call(routed_own_kernel, out_shape=(pltpu.VMEM((chips, 8, units...  3.43 us
    pallas_call x1, Pallas kernels, dispatch(): pl.pallas_call(dispatch_kernel, out_shape=jax.ShapeDtypeStruct((chips * 8...  2.16 us
    ppermute x1, starting transfers between devices, shards(): lax.ppermute(mine, 'y', [(y, (y + ring // 2) % ring) for y in range(ring)])  1.96 us
  transfers between devices with their start and end apart: 7, of which 3 were waited for; matrix products, arithmetic and copies ran while one was open for 0% of the time, Pallas kernels for 22%

profile of v5, /device:TPU:1, one launch (start us, length us, event | category | flops | bytes accessed | tf_op | source)
XLA Modules:
  0.0 65.3 jit_solution(13280676717779902209)
XLA Ops:
  0.6 0.0 copy-start.2
  0.6 0.0 copy-start
  0.7 1.5 %collective-permute-start = (bf16[48,2560]{1,0:T(8,128)(2,1)}, bf16[48,2560]{1,0:T(8,128)(2,1)S(1)}, u32[]{:S(2)}, u32[]{:S(2)}) collective-permute-start(bf16[48,2560]{1,0:T(8,128)(2,1)} %refs_0_.1), channel_id=1, source_target_pairs={{0,1},{1,0},{2,3},{3,2},{4,5},{5,4},{6,7},{7,6},{8,9},{9,8},{10,11... | collective-permute-start | bytes 737288 | tf_op jit(solution)/shard_map/ppermute | solution.py:281
  2.2 2.2 %dispatch.1 = bf16[512,640]{1,0:T(8,128)(2,1)S(1)} custom-call(bf16[48,2560]{1,0:T(8,128)(2,1)} %refs_0_.1, f32[48]{0:T(128)} %scores_ref.1, s32[48]{0:T(128)} %ids_ref.3), custom_call_target="tpu_custom_call" | custom-call | flops 20000000000 | bytes 2000000 | tf_op jit(solution)/shard_map/dispatch/pallas_call | solution.py:45
  4.3 0.0 collective-permute-done.partner_ref.refs_1_
  4.3 25.1 %all_to_all.10 = bf16[64,8,640]{2,1,0:T(8,128)(2,1)S(1)} all-to-all(bf16[64,8,640]{2,1,0:T(8,128)(2,1)S(1)} %bitcast.13), channel_id=1, replica_groups=mesh['wide'=16,'y'=4,'core'=2] {'wide','y'}, dimensions={0} | all-to-all | bytes 1310720 | tf_op jit(solution)/shard_map/all_to_all | solution.py:295
  29.4 1.5 %collective-permute-start.1 = (bf16[512,640]{1,0:T(8,128)(2,1)S(1)}, bf16[512,640]{1,0:T(8,128)(2,1)S(1)}, u32[]{:S(2)}, u32[]{:S(2)}) collective-permute-start(bf16[512,640]{1,0:T(8,128)(2,1)S(1)} %bitcast.10), channel_id=1, source_target_pairs={{0,1},{1,0},{2,3},{3,2},{4,5},{5,4},{6,7},{7,6},{8,9},{9,8},{10,11... | collective-permute-start | bytes 1966088 | tf_op jit(solution)/shard_map/ppermute | solution.py:281
  30.9 3.4 %routed_own.1 = (bf16[64,8,512]{2,1,0:T(8,128)(2,1)S(1)}, bf16[2,48,2560]{2,1,0:T(8,128)(2,1)}) custom-call(bf16[512,640]{1,0:T(8,128)(2,1)S(1)} %bitcast.11, bf16[2560,2048]{1,0:T(8,128)(2,1)S(1)} %bitcast.6, bf16[2560,2048]{1,0:T(8,128)(2,1)S(1)} %bitcast.8, bf16[48,2560]{1,0:T(8,128)(2,1)S(1)} %copy-done.2, ...), custom_call_target="tpu_custom_call" | custom-call | flops 2684354560 | bytes 1000000 | tf_op jit(solution)/shard_map/routed_own/pallas_call | solution.py:162
  34.3 0.3 collective-permute-start.2
  34.7 2.0 %collective-permute-start.3 = (bf16[48,2560]{1,0:T(8,128)(2,1)S(1)}, bf16[48,2560]{1,0:T(8,128)(2,1)S(1)}, u32[]{:S(2)}, u32[]{:S(2)}) collective-permute-start(bf16[48,2560]{1,0:T(8,128)(2,1)S(1)} %copy-done.2), channel_id=1, source_target_pairs={{0,4},{2,6},{4,0},{6,2},{1,5},{3,7},{5,1},{7,3},{8,12},{10,14},{12... | collective-permute-start | bytes 737288 | tf_op jit(solution)/shard_map/ppermute | solution.py:302
  36.6 0.0 collective-permute-done.1.other_ref
  36.6 4.3 %routed_other.1 = bf16[64,2,8,512]{3,2,1,0:T(8,128)(2,1)} custom-call(bf16[512,640]{1,0:T(8,128)(2,1)S(1)} %collective-permute-done.1.other_ref, bf16[64,8,512]{2,1,0:T(8,128)(2,1)S(1)} %get-tuple-element.16.mine_ref, bf16[2560,2048]{1,0:T(8,128)(2,1)S(1)} %bitcast.7, bf16[2560,2048]{1,0:T(8,128)(2,1)S(1)} %bitcast.9), custom_call_target="tpu_custom_call" | custom-call | flops 2684354560 | bytes 1000000 | tf_op jit(solution)/shard_map/routed_other/pallas_call | solution.py:182
  40.9 0.0 copy-start.3
  40.9 4.0 %all-to-all-start.1 = ((bf16[128,8,512]{2,1,0:T(8,128)(2,1)}), bf16[128,8,512]{2,1,0:T(8,128)(2,1)S(1)}, u32[]{:S(2)}, u32[]{:S(2)}) async-start(bf16[128,8,512]{2,1,0:T(8,128)(2,1)} %bitcast.4), calls=%async_computation.1 | async-start | bytes 2097152 | tf_op jit(solution)/shard_map/all_to_all | solution.py:306
  44.9 0.0 collective-permute-done.3.refs_4_
  45.0 0.3 collective-permute-done.2.refs_2_
  45.2 11.2 %collective-permute-start.4 = (bf16[2,48,2560]{2,1,0:T(8,128)(2,1)S(1)}, bf16[2,48,2560]{2,1,0:T(8,128)(2,1)S(1)}, u32[]{:S(2)}, u32[]{:S(2)}) collective-permute-start(bf16[2,48,2560]{2,1,0:T(8,128)(2,1)S(1)} %collective-permute-done.2.refs_2_), channel_id=1, source_target_pairs={{0,1},{1,0},{2,3},{3,2},{4,5},{5,4},{6,7},{7,6},{8,9},{9,8},{10,11... | collective-permute-start | bytes 1474568 | tf_op jit(solution)/shard_map/ppermute | solution.py:281
  56.5 0.0 collective-permute-start.5
  56.5 1.8 %collective-permute-done.5.refs_5_ = bf16[48,2560]{1,0:T(8,128)(2,1)S(1)} collective-permute-done((bf16[48,2560]{1,0:T(8,128)(2,1)S(1)}, bf16[48,2560]{1,0:T(8,128)(2,1)S(1)}, u32[]{:S(2)}, u32[]{:S(2)}) %collective-permute-start.5) | collective-permute-done | bytes 245792 | tf_op jit(solution)/shard_map/ppermute | solution.py:281
  58.3 0.0 collective-permute-done.4.refs_3_
  58.3 4.8 %shared.1 = bf16[384,512]{1,0:T(8,128)(2,1)} custom-call(bf16[48,2560]{1,0:T(8,128)(2,1)S(1)} %copy-done.2, bf16[48,2560]{1,0:T(8,128)(2,1)S(1)} %collective-permute-done.partner_ref.refs_1_, bf16[2,48,2560]{2,1,0:T(8,128)(2,1)S(1)} %collective-permute-done.2.refs_2_, bf16[2,48,2560]{2,1,0:T(8,128)(2,1)S(1)} %collective-permute-done.4.refs_3_, ...), custom_call_target="tpu_custom_call" | custom-call | flops 5000000000 | bytes 8000000 | tf_op jit(solution)/shard_map/shared/pallas_call | solution.py:229
  63.2 0.7 %all-to-all-done.1 = bf16[128,8,512]{2,1,0:T(8,128)(2,1)S(1)} async-done(((bf16[128,8,512]{2,1,0:T(8,128)(2,1)}), bf16[128,8,512]{2,1,0:T(8,128)(2,1)S(1)}, u32[]{:S(2)}, u32[]{:S(2)}) %all-to-all-start.1) | async-done | bytes 1048608 | tf_op jit(solution)/shard_map/all_to_all | solution.py:306
  63.8 0.0 copy-done.3
  63.9 1.5 %collect.1 = bf16[48,4096]{1,0:T(8,128)(2,1)} custom-call(bf16[1024,512]{1,0:T(8,128)(2,1)S(1)} %bitcast.12, s32[48]{0:T(128)S(1)} %copy-done.3), custom_call_target="tpu_custom_call" | custom-call | flops 400000000 | bytes 1500000 | tf_op jit(solution)/shard_map/collect/pallas_call | solution.py:271
  (4 shorter events, 0.0 us)
Async XLA Ops:
  0.6 30.3 %copy-start.2 = (bf16[48,2560]{1,0:T(8,128)(2,1)S(1)}, bf16[48,2560]{1,0:T(8,128)(2,1)}, u32[]{:S(2)}) copy-start(bf16[48,2560]{1,0:T(8,128)(2,1)} %refs_0_.1) | copy-start | bytes 737284
  0.6 30.3 %copy-start = (bf16[1,2560,2048]{2,1,0:T(8,128)(2,1)S(1)}, bf16[1,2560,2048]{2,1,0:T(8,128)(2,1)}, u32[]{:S(2)}) copy-start(bf16[1,2560,2048]{2,1,0:T(8,128)(2,1)} %param.10) | copy-start | bytes 31457284
  0.7 30.3 %copy-start.1 = (bf16[1,2560,2048]{2,1,0:T(8,128)(2,1)S(1)}, bf16[1,2560,2048]{2,1,0:T(8,128)(2,1)}, u32[]{:S(2)}) copy-start(bf16[1,2560,2048]{2,1,0:T(8,128)(2,1)} %param.11) | copy-start | bytes 31457284
  0.7 3.7 %collective-permute-start = (bf16[48,2560]{1,0:T(8,128)(2,1)}, bf16[48,2560]{1,0:T(8,128)(2,1)S(1)}, u32[]{:S(2)}, u32[]{:S(2)}) collective-permute-start(bf16[48,2560]{1,0:T(8,128)(2,1)} %refs_0_.1), channel_id=1, source_target_pairs={{0,1},{1,0},{2,3},{3,2},{4,5},{5,4},{6,7},{7,6},{8,9},{9,8},{10,11... | collective-permute-start | bytes 737288 | tf_op jit(solution)/shard_map/ppermute | solution.py:281
  29.4 7.2 %collective-permute-start.1 = (bf16[512,640]{1,0:T(8,128)(2,1)S(1)}, bf16[512,640]{1,0:T(8,128)(2,1)S(1)}, u32[]{:S(2)}, u32[]{:S(2)}) collective-permute-start(bf16[512,640]{1,0:T(8,128)(2,1)S(1)} %bitcast.10), channel_id=1, source_target_pairs={{0,1},{1,0},{2,3},{3,2},{4,5},{5,4},{6,7},{7,6},{8,9},{9,8},{10,11... | collective-permute-start | bytes 1966088 | tf_op jit(solution)/shard_map/ppermute | solution.py:281
  34.3 10.9 %collective-permute-start.2 = (bf16[2,48,2560]{2,1,0:T(8,128)(2,1)}, bf16[2,48,2560]{2,1,0:T(8,128)(2,1)S(1)}, u32[]{:S(2)}, u32[]{:S(2)}) collective-permute-start(bf16[2,48,2560]{2,1,0:T(8,128)(2,1)} %get-tuple-element.17), channel_id=1, source_target_pairs={{0,2},{1,7},{2,4},{3,1},{4,6},{5,3},{6,0},{7,5},{8,10},{9,15},{10,... | collective-permute-start | bytes 1474568 | tf_op jit(solution)/shard_map/ppermute | solution.py:286
  34.7 10.3 %collective-permute-start.3 = (bf16[48,2560]{1,0:T(8,128)(2,1)S(1)}, bf16[48,2560]{1,0:T(8,128)(2,1)S(1)}, u32[]{:S(2)}, u32[]{:S(2)}) collective-permute-start(bf16[48,2560]{1,0:T(8,128)(2,1)S(1)} %copy-done.2), channel_id=1, source_target_pairs={{0,4},{2,6},{4,0},{6,2},{1,5},{3,7},{5,1},{7,3},{8,12},{10,14},{12... | collective-permute-start | bytes 737288 | tf_op jit(solution)/shard_map/ppermute | solution.py:302
  40.9 23.0 %copy-start.3 = (s32[48]{0:T(128)S(1)}, s32[48]{0:T(128)}, u32[]{:S(2)}) copy-start(s32[48]{0:T(128)} %ids_ref.3) | copy-start | bytes 580
  40.9 22.9 %all-to-all-start.1 = ((bf16[128,8,512]{2,1,0:T(8,128)(2,1)}), bf16[128,8,512]{2,1,0:T(8,128)(2,1)S(1)}, u32[]{:S(2)}, u32[]{:S(2)}) async-start(bf16[128,8,512]{2,1,0:T(8,128)(2,1)} %bitcast.4), calls=%async_computation.1 | async-start | bytes 2097152 | tf_op jit(solution)/shard_map/all_to_all | solution.py:306
  45.2 13.1 %collective-permute-start.4 = (bf16[2,48,2560]{2,1,0:T(8,128)(2,1)S(1)}, bf16[2,48,2560]{2,1,0:T(8,128)(2,1)S(1)}, u32[]{:S(2)}, u32[]{:S(2)}) collective-permute-start(bf16[2,48,2560]{2,1,0:T(8,128)(2,1)S(1)} %collective-permute-done.2.refs_2_), channel_id=1, source_target_pairs={{0,1},{1,0},{2,3},{3,2},{4,5},{5,4},{6,7},{7,6},{8,9},{9,8},{10,11... | collective-permute-start | bytes 1474568 | tf_op jit(solution)/shard_map/ppermute | solution.py:281
  56.5 1.8 %collective-permute-start.5 = (bf16[48,2560]{1,0:T(8,128)(2,1)S(1)}, bf16[48,2560]{1,0:T(8,128)(2,1)S(1)}, u32[]{:S(2)}, u32[]{:S(2)}) collective-permute-start(bf16[48,2560]{1,0:T(8,128)(2,1)S(1)} %collective-permute-done.3.refs_4_), channel_id=1, source_target_pairs={{0,1},{1,0},{2,3},{3,2},{4,5},{5,4},{6,7},{7,6},{8,9},{9,8},{10,11... | collective-permute-start | bytes 737288 | tf_op jit(solution)/shard_map/ppermute | solution.py:281
